TPU v7x, 32 devices: a whole 2x2x4 slice. The times are simulated.
32 devices in a mesh: week: 4 (over x, core), row: 4 (over z), col: 2 (over y).
Axes of the slice: x: 2, y: 2, z: 4, core: 2. Of those that a mesh axis runs over, the one named last changes fastest.
Arguments:
- sensitivity: bfloat16 [4, 3, 1024, 4096], P('week', None, None, ('row', 'col')), may hold values from -0.1875 to 0.1875
- reach: int32 [4, 1024], P('week'), may hold values from 0 to 2, as said below
- obs_weight: float32 [4, 1024], P('week'), may hold values from 0.25 to 4
- prior_precision: float32 [4, 4096], P('week', ('row', 'col')), may hold values from 0.5 to 4
- pivot_solve: bfloat16 [4096, 4096], P('week', ('row', 'col')), may hold values from -0.09375 to 0.09375
Outputs:
- hessian_band: float32 [4, 3, 4096, 4096], P('week', None, ('row', 'col'))
- panel: bfloat16 [4096, 4096], P(('row', 'col'), 'week')
- schur: float32 [4096, 4096], P(('row', 'col'), 'week')
Inputs may be any that keep to these rules, and one draw needn't show every extreme that they name: The number of observations at each reach differs widely from week to week; in some week w >= 2 every observation has reach 2.
All inputs are finite; a program needn't handle non-finite values.
Results may differ from a plain program's by a relative error of at most 0.013.
Values may be sent and summed in bfloat16 or wider, within the bound.
A program may use at most 128 MiB of HBM per device.

v0:
```python
import functools

import jax
import jax.numpy as jnp
from jax import lax
from jax.experimental import pallas as pl
from jax.experimental.pallas import tpu as pltpu
from jax.sharding import PartitionSpec as P

ROW, COL, WEEK = "row", "col", "week"
DMA = pltpu.SemaphoreType.DMA

UNITS = 5
UNIT_SLOT = ((0, 0, 0, 0), (0, 0, 0, 0), (1, 1, 3, 3), (1, 2, 2, 3), (2, 0, 0, 2))
UNIT_HALF = ((0, 0, 0, 0), (1, 1, 1, 1), (0, 0, 1, 0), (1, 0, 1, 1), (0, 0, 0, 1))
LOCAL = {
    0: ((0, 0),) * 4,
    1: ((0, 1),) * 4,
    2: (None, None, (1, 1), (1, 0)),
    3: (None, None, (2, 1), (1, 1)),
    4: (None, None, None, (2, 1)),
}
FIRST = ((1, 1, 0, 0, 2), (1, 1, 1, 0, 3), (2, 2, 0, 0, 4), (2, 1, 0, 1, 2), (3, 2, 0, 1, 3))
ONWARD = (
    ((2, 1, 3, 0), (3, 1, 3, 1), (4, 1, 4, 2), (4, 2, 2, 4)),
    ((2, 2, 3, 3), (3, 3, 2, 0)),
    ((2, 1, 1, 3), (3, 0, 2, 0)),
    ((2, 2, 1, 0), (3, 2, 1, 1), (4, 2, 4, 2), (4, 1, 2, 4)),
)
RELAY = {0: (1, 1, 4), 3: (0, 2, 4)}
FLOWS = 6


def pick(week, values):
    out = jnp.int32(values[0])
    for k, value in enumerate(values[1:], 1):
        out = jnp.where(week == k, jnp.int32(value), out)
    return out


def gather_kernel(n_row, n_col, x_ref, f_ref, own, put_sem, first_s, first_r, main_s, main_r, band_s, band_r,
                  side_s, side_r, rest_s, rest_r, pass_s, pass_r, flow_s, flow_r):
    row, col, week = lax.axis_index(ROW), lax.axis_index(COL), lax.axis_index(WEEK)
    _, length, width = x_ref.shape
    half = length // 2
    band = max(half * 5 // 32 // 16 * 16, 16)
    n = n_row * n_col
    peers = range(1, n_col)
    n_week = 4
    has = (row < n_row - 1, row > 0)
    target = (lax.rem(row + 1, n_row), lax.rem(row + n_row - 1, n_row))

    barrier = pltpu.get_barrier_semaphore()
    for d in range(2):
        pl.semaphore_signal(barrier, inc=1, device_id={ROW: target[d]})
    for k in peers:
        pl.semaphore_signal(barrier, inc=1, device_id={COL: lax.rem(col + k, n_col)})
    for k in range(1, n_week):
        pl.semaphore_signal(barrier, inc=1, device_id={WEEK: lax.rem(week + k, n_week)})
    pl.semaphore_wait(barrier, 2 + (n_col - 1) + (n_week - 1))

    slots = [pick(week, UNIT_SLOT[u]) for u in range(UNITS)]
    starts = [pl.multiple_of(pick(week, UNIT_HALF[u]) * half, half) for u in range(UNITS)]

    def slab(at_row, at_col):
        return at_row * n_col + at_col

    def cell(slot, start, s, first=0, count=half):
        at = pl.ds(pl.multiple_of(s * width, width), width)
        return f_ref.at[slot, pl.ds(pl.multiple_of(start + first, 16), count), at]

    def place(u, s, first=0, count=half):
        return cell(slots[u], starts[u], s, first, count)

    def active(u, body):
        if u < 4:
            body()
        else:
            pl.when((week == 0) | (week == n_week - 1))(body)

    def origin(step, d):
        return lax.rem(row + n_row - step if d == 0 else row + step, n_row)

    def arrives(step, d):
        return row >= step if d == 0 else row + step < n_row

    def other(k):
        return lax.rem(col + n_col - k, n_col)

    def remote(ref, s_sem, r_sem, device, to=None):
        return pltpu.make_async_remote_copy(ref, ref if to is None else to, s_sem, r_sem, device_id=device)

    def main(u, step, d):
        return remote(place(u, slab(origin(step, d), col)), main_s.at[u, step, d], main_r.at[u, step, d],
                      {ROW: target[d]})

    def strip(u, step, d, k):
        return remote(place(u, slab(origin(step, d), other(k)), 0, band), band_s.at[u, step, d, k - 1],
                      band_r.at[u, step, d, k - 1], {ROW: target[d]})

    def side(u, k):
        return remote(place(u, slab(row, col), 0, band), side_s.at[u, k - 1], side_r.at[u, k - 1],
                      {COL: lax.rem(col + k, n_col)})

    def rest(u, k):
        return remote(place(u, slab(row, col), band, half - band), rest_s.at[u, k - 1], rest_r.at[u, k - 1],
                      {COL: lax.rem(col + k, n_col)})

    def onward(u, step, d, k):
        return remote(place(u, slab(origin(step, d), col), band, half - band), pass_s.at[u, step - 1, d, k - 1],
                      pass_r.at[u, step - 1, d, k - 1], {COL: lax.rem(col + k, n_col)})

    def flows(w, u, s):
        sent = 0
        for i, (unit, to_week, to_slot, flow) in enumerate(ONWARD[w]):
            if unit == u:
                start = UNIT_HALF[u][w] * half
                yield remote(cell(UNIT_SLOT[u][w], start, s), flow_s.at[i, s], flow_r.at[flow, s],
                             {WEEK: jnp.int32(to_week)}, cell(to_slot, start, s))

    def spread(u, s, act="start"):
        for w in range(n_week):
            if any(unit == u for unit, *_ in ONWARD[w]):
                @pl.when(week == w)
                def _(w=w):
                    for copy in flows(w, u, s):
                        copy.start() if act == "start" else copy.wait_send()

    def relay(s, act):
        for w, (h, to_week, to_slot) in RELAY.items():
            @pl.when(week == w)
            def _(w=w, h=h, to_week=to_week, to_slot=to_slot):
                ref = cell(2, h * half, s)
                copy = remote(ref, flow_s.at[4, s], flow_r.at[5, s], {WEEK: jnp.int32(to_week)},
                              cell(to_slot, h * half, s))
                if act == "start":
                    remote(ref, flow_s.at[0, s], flow_r.at[0, s], {WEEK: jnp.int32(to_week)}).wait_recv()
                    copy.start()
                else:
                    copy.wait_send()

    mine = slab(row, col)

    def first(act):
        for i, (w, lag, h, to_week, u) in enumerate(FIRST):
            @pl.when(week == w)
            def _(w=w, lag=lag, h=h, to_week=to_week, u=u):
                copy = remote(x_ref.at[lag, pl.ds(h * half, half), :], first_s.at[u], first_r.at[u],
                              {WEEK: jnp.int32(to_week)}, cell(UNIT_SLOT[u][to_week], h * half, mine))
                copy.start() if act == "start" else copy.wait_send()

    def take(u, w):
        lag, h = LOCAL[u][w]
        return pltpu.make_async_copy(x_ref.at[lag, pl.ds(h * half, half), :], own.at[u], put_sem.at[u])

    def put(u):
        return pltpu.make_async_copy(own.at[u], place(u, mine), put_sem.at[u])

    def local(u, body):
        groups = {}
        for w in range(n_week):
            groups.setdefault(LOCAL[u][w], []).append(w)
        for what, weeks in groups.items():
            if what is None:
                continue
            if len(weeks) == n_week:
                body(weeks[0])
            else:
                for w in weeks:
                    pl.when(week == w)(functools.partial(body, w))

    first("start")
    for u in range(UNITS):
        local(u, lambda w, u=u: take(u, w).start())
    for u in range(UNITS):
        def move(w, u=u):
            take(u, w).wait()
            put(u).start()

        local(u, move)

    def begin(u):
        local(u, lambda w: put(u).wait())
        for _, _, _, to_week, unit in FIRST:
            if unit == u:
                @pl.when(week == to_week)
                def _():
                    remote(place(u, mine), first_s.at[u], first_r.at[u], {ROW: target[0]}).wait_recv()

        def go():
            for k in peers:
                side(u, k).start()
            for d in range(2):
                pl.when(has[d])(lambda d=d: main(u, 0, d).start())
            for k in peers:
                rest(u, k).start()

        active(u, go)
        spread(u, mine)

    for u in range(UNITS):
        begin(u)

    for u in range(UNITS):
        def spread_band(u=u):
            for k in peers:
                side(u, k).wait_recv()
                for d in range(2):
                    pl.when(has[d])(lambda d=d, k=k: strip(u, 0, d, k).start())

        active(u, spread_band)

    def across(step):
        for u in range(UNITS):
            if step == 0:
                def body(u=u):
                    for k in peers:
                        rest(u, k).wait_recv()
                        spread(u, slab(row, other(k)))

                active(u, body)
            else:
                for d in range(2):
                    def body(u=u, d=d):
                        for k in peers:
                            onward(u, step, d, k).wait_recv()
                            spread(u, slab(origin(step, d), other(k)))

                    active(u, lambda d=d, body=body: pl.when(arrives(step, d))(body))

    def relays(step, act):
        if step == 0:
            relay(mine, act)
            for k in peers:
                relay(slab(row, other(k)), act)
        else:
            for d in range(2):
                @pl.when(arrives(step, d))
                def _(d=d):
                    relay(slab(origin(step, d), col), act)
                    for k in peers:
                        relay(slab(origin(step, d), other(k)), act)

    for step in range(1, n_row):
        for u in range(UNITS):
            for d in range(2):
                def advance(u=u, d=d, step=step):
                    main(u, step - 1, d).wait_recv()
                    if step < n_row - 1:
                        pl.when(has[d])(lambda: main(u, step, d).start())
                    for k in peers:
                        onward(u, step, d, k).start()
                    spread(u, slab(origin(step, d), col))
                    for k in peers:
                        strip(u, step - 1, d, k).wait_recv()
                        if step < n_row - 1:
                            pl.when(has[d])(lambda k=k: strip(u, step, d, k).start())

                active(u, lambda d=d, step=step, advance=advance: pl.when(arrives(step, d))(advance))
        across(step - 1)
        if step > 1:
            relays(step - 2, "start")
    across(n_row - 1)
    for step in range(max(n_row - 2, 0), n_row):
        relays(step, "start")

    @pl.when((week == 1) | (week == 2))
    def _():
        for s in range(n):
            for flow in range(FLOWS):
                ref = cell(0, 0, s)
                remote(ref, flow_s.at[0, s], flow_r.at[flow, s], {ROW: target[0]}).wait_recv()

    first("wait")
    for u in range(UNITS):
        def finish(u=u):
            for k in peers:
                side(u, k).wait_send()
                rest(u, k).wait_send()
            for d in range(2):
                @pl.when(has[d])
                def _(d=d):
                    main(u, 0, d).wait_send()
                    for k in peers:
                        strip(u, 0, d, k).wait_send()
                for step in range(1, n_row):
                    @pl.when(arrives(step, d))
                    def _(d=d, step=step):
                        for k in peers:
                            onward(u, step, d, k).wait_send()
                        if step < n_row - 1:
                            @pl.when(has[d])
                            def _():
                                main(u, step, d).wait_send()
                                for k in peers:
                                    strip(u, step, d, k).wait_send()

        active(u, finish)
        if u >= 2:
            for s in range(n):
                spread(u, s, "wait")
    for s in range(n):
        relay(s, "wait")


def gather(x, collective_id):
    n_row, n_col = lax.axis_size(ROW), lax.axis_size(COL)
    _, length, width = x.shape
    n = n_row * n_col
    kinds = (UNITS, n_row - 1, 2)
    wide = (*kinds, n_col - 1)
    sides = (UNITS, n_col - 1)
    sent = length * width * 2 * (n - 1) * 9 // 4
    return pl.pallas_call(
        functools.partial(gather_kernel, n_row, n_col),
        out_shape=jax.ShapeDtypeStruct((5, length, width * n), x.dtype),
        in_specs=[pl.BlockSpec(memory_space=pl.ANY)],
        out_specs=pl.BlockSpec(memory_space=pl.ANY),
        scratch_shapes=[
            pltpu.VMEM((UNITS, length // 2, width), x.dtype), DMA((UNITS,)), DMA((UNITS,)), DMA((UNITS,)),
            DMA(kinds), DMA(kinds), DMA(wide), DMA(wide), DMA(sides), DMA(sides), DMA(sides), DMA(sides),
            DMA(wide), DMA(wide), DMA((5, n)), DMA((FLOWS, n)),
        ],
        compiler_params=pltpu.CompilerParams(collective_id=collective_id, has_side_effects=True),
        cost_estimate=pl.CostEstimate(flops=0, bytes_accessed=sent * 8, transcendentals=0),
    )(x)


def exchange_kernel(x_ref, e_ref, own, put_sem, send, recv):
    week = lax.axis_index(WEEK)
    n_week = 4
    barrier = pltpu.get_barrier_semaphore()
    for k in range(1, n_week):
        pl.semaphore_signal(barrier, inc=1, device_id={WEEK: lax.rem(week + k, n_week)})
    pl.semaphore_wait(barrier, n_week - 1)
    roles = ((1, ((1, 2), (0, 0)), 0, 2), (2, ((2, 3), (1, 1)), 3, 1))

    def copy(src, place, to, sem):
        return pltpu.make_async_remote_copy(src, e_ref.at[place], send.at[place, sem], recv.at[place],
                                            device_id={WEEK: jnp.int32(to)})

    for w, items, near, far in roles:
        @pl.when(week == w)
        def _(w=w, items=items, near=near, far=far):
            for lag, at in items:
                copy(x_ref.at[lag], at, far, 0).start()
            for lag, at in items:
                copy(x_ref.at[lag], at, near, 1).start()
                pltpu.make_async_copy(x_ref.at[lag], own.at[lag], put_sem.at[lag]).start()
            for lag, at in items:
                pltpu.make_async_copy(x_ref.at[lag], own.at[lag], put_sem.at[lag]).wait()
                pltpu.make_async_copy(own.at[lag], e_ref.at[at], put_sem.at[lag]).start()
            theirs = roles[2 - w][1]
            for _, at in theirs:
                copy(e_ref.at[at], at, near, 0).wait_recv()
                copy(e_ref.at[at], at, near, 0).start()
            for lag, at in items:
                copy(x_ref.at[lag], at, far, 0).wait_send()
                copy(x_ref.at[lag], at, near, 1).wait_send()
                pltpu.make_async_copy(own.at[lag], e_ref.at[at], put_sem.at[lag]).wait()
            for _, at in theirs:
                copy(e_ref.at[at], at, near, 0).wait_send()

    @pl.when((week == 0) | (week == n_week - 1))
    def _():
        for at in range(4):
            copy(e_ref.at[at], at, 0, 0).wait_recv()


def exchange(x, collective_id):
    _, length, width = x.shape
    return pl.pallas_call(
        exchange_kernel,
        out_shape=jax.ShapeDtypeStruct((4, length, width), x.dtype),
        in_specs=[pl.BlockSpec(memory_space=pl.ANY)],
        out_specs=pl.BlockSpec(memory_space=pl.ANY),
        scratch_shapes=[pltpu.VMEM(x.shape, x.dtype), DMA((3,)), DMA((4, 2)), DMA((4,))],
        compiler_params=pltpu.CompilerParams(collective_id=collective_id, has_side_effects=True),
    )(x)


PRODUCTS = ((0, 0, 0, (0, 3)), (0, 1, 1, (0, 2)), (0, 2, 2, (0, 1)), (1, 0, 3, (1, 3)), (1, 1, 4, (1, 2)),
            (2, 0, 2, (2, 3)))


def bands_kernel(at_ref, left_ref, weight_ref, prior_ref, full_ref, out_ref, turned):
    week, mine = at_ref[0], at_ref[1]
    tile = pl.program_id(0)
    width = left_ref.shape[2]
    columns = full_ref.shape[2]

    @pl.when(tile == 0)
    def _():
        for p, (_, slot, _, (lo, hi)) in enumerate(PRODUCTS):
            @pl.when((week >= lo) & (week <= hi))
            def _(p=p, slot=slot):
                flat = left_ref[slot].T.astype(jnp.float32) * weight_ref[p][None, :]
                turned[p] = flat.astype(turned.dtype)

    out_ref[...] = jnp.zeros_like(out_ref)
    for p, (band, _, slot, (lo, hi)) in enumerate(PRODUCTS):
        @pl.when((week >= lo) & (week <= hi))
        def _(p=p, band=band, slot=slot):
            out_ref[band] += jnp.dot(turned[p], full_ref[slot], preferred_element_type=jnp.float32)

    row_ids = lax.broadcasted_iota(jnp.int32, (width, columns), 0) + mine * width
    col_ids = lax.broadcasted_iota(jnp.int32, (width, columns), 1) + tile * columns
    out_ref[0] += jnp.where(row_ids == col_ids, prior_ref[:, :1], 0.0)


def bands(at, full, weights, prior):
    slots, length, regions = full.shape
    width = prior.shape[0]
    columns = min(512, regions)
    return pl.pallas_call(
        bands_kernel,
        out_shape=jax.ShapeDtypeStruct((3, width, regions), jnp.float32),
        grid_spec=pltpu.PrefetchScalarGridSpec(
            num_scalar_prefetch=1,
            grid=(regions // columns,),
            in_specs=[
                pl.BlockSpec((3, length, width), lambda j, at: (0, 0, at[1]), pipeline_mode=pl.Buffered(1)),
                pl.BlockSpec(weights.shape, lambda j, at: (0, 0)),
                pl.BlockSpec(prior.shape, lambda j, at: (0, 0)),
                pl.BlockSpec((slots, length, columns), lambda j, at: (0, 0, j)),
            ],
            out_specs=pl.BlockSpec((3, width, columns), lambda j, at: (0, 0, j)),
            scratch_shapes=[pltpu.VMEM((len(PRODUCTS), width, length), full.dtype)],
        ),
        compiler_params=pltpu.CompilerParams(dimension_semantics=("arbitrary",), vmem_limit_bytes=60 << 20),
        cost_estimate=pl.CostEstimate(
            flops=10 * width * length * regions, bytes_accessed=full.size * 2 + 12 * width * regions,
            transcendentals=0),
    )(at, full, weights, prior, full)


def contract_first(left, right):
    return lax.dot_general(left, right, (((0,), (0,)), ((), ())), preferred_element_type=jnp.float32)


def contract_last(left, right):
    return lax.dot_general(left, right, (((1,), (1,)), ((), ())), preferred_element_type=jnp.float32)


def body(sensitivity, reach, obs_weight, prior_precision, pivot_solve):
    week = lax.axis_index(WEEK)
    n_week, n_row, n_col = (lax.axis_size(name) for name in (WEEK, ROW, COL))
    assert n_week == 4
    local = sensitivity[0]
    lags, length, width = local.shape
    mine = lax.axis_index(ROW) * n_col + lax.axis_index(COL)

    lag = jnp.arange(lags)[:, None]
    own_weight = jnp.where((reach >= lag) & (week >= lag), obs_weight, 0.0)
    by_week = lax.all_gather(own_weight, WEEK)
    later = jnp.concatenate([by_week, jnp.zeros((lags, lags, length), by_week.dtype)])
    here = lax.dynamic_slice(later, (week, 0, 0), (lags, lags, length))
    weights = jnp.stack([here[0, 0], here[1, 1], here[2, 2], here[0, 1], here[1, 2], here[0, 2]])

    near = exchange(local, 1)
    low = jnp.concatenate([near[2], near[3]])
    part = contract_last(low, pivot_solve).astype(jnp.bfloat16)
    whole = lax.psum(part, (ROW, COL))
    part, local = lax.optimization_barrier((part, local))
    full = gather(local, 0)
    panel_weight = jnp.concatenate([by_week[1, 1], by_week[2, 2]])
    left = (panel_weight[:, None] * near[:2].reshape(2 * length, width).astype(jnp.float32)).astype(jnp.bfloat16)
    panel = contract_first(left, whole).astype(jnp.bfloat16)
    inner = contract_last(panel, whole).astype(jnp.bfloat16)
    inner = lax.psum(inner, WEEK)

    at = jnp.stack([week, mine]).astype(jnp.int32)
    prior = jnp.broadcast_to(prior_precision[0][:, None], (width, 128))
    h = bands(at, full, weights, prior)

    right = (inner.astype(jnp.float32) * panel_weight).astype(jnp.bfloat16)
    spent = right.shape[0]
    out = h[0] - (jnp.dot(right[:, :length], full[0], preferred_element_type=jnp.float32)
                  + jnp.dot(right[:, length:], full[1], preferred_element_type=jnp.float32))
    out = out.astype(jnp.bfloat16)
    quarter = out.shape[1] // n_week
    schur = out[:, quarter : 2 * quarter]
    for w in (0, 2, 3):
        moved = lax.ppermute(out[:, w * quarter : (w + 1) * quarter], WEEK, [(1, w)])
        schur = jnp.where(week == w, moved, schur)
    return (h[None], panel, schur.astype(jnp.float32))


def solution(mesh):
    placed = (
        P(WEEK, None, None, (ROW, COL)),
        P(WEEK, None),
        P(WEEK, None),
        P(WEEK, (ROW, COL)),
        P(WEEK, (ROW, COL)),
    )
    return jax.shard_map(
        body,
        mesh=mesh,
        in_specs=placed,
        out_specs=(
            P(WEEK, None, (ROW, COL), None),
            P((ROW, COL), WEEK),
            P((ROW, COL), WEEK),
        ),
        check_vma=False,
    )
```

profile of v0, /device:TPU:5, one launch (start us, length us, event | category | flops | bytes accessed | tf_op | source)
XLA Modules:
  0.0 495.0 jit_solution(7907811272991431418)
XLA Ops:
  7.2 0.0 copy-start
  7.2 0.0 all-reduce.4.cloned.1.call-start
  7.2 29.1 %shard_map.76 = bf16[4,1024,512]{2,1,0:T(8,128)(2,1)} custom-call(bf16[3,1024,512]{2,1,0:T(8,128)(2,1)} %bitcast.47), custom_call_target="tpu_custom_call" | custom-call | tf_op jit(solution)/shard_map/pallas_call | solution.py:372
  36.4 1.7 slice_bitcast_fusion.2
  38.1 4.4 convolution_convert_fusion
  42.5 0.0 all-reduce.4.cloned.1.call-update
  42.5 0.0 all-reduce.6.cloned.1.call-start
  42.6 0.0 copy-start.3
  42.6 324.8 %shard_map.77.left_ref.full_ref = bf16[5,1024,4096]{2,1,0:T(8,128)(2,1)} custom-call(bf16[3,1024,512]{2,1,0:T(8,128)(2,1)} %bitcast.48), custom_call_target="tpu_custom_call" | custom-call | bytes 132120576 | tf_op jit(solution)/shard_map/pallas_call | solution.py:314
  367.5 0.1 fusion.26
  367.6 4.1 all_gather.4
  371.7 0.7 stack.15.weight_ref
  372.3 0.6 pad_add_fusion.at_ref
  372.9 4.8 fusion.17
  377.7 0.0 copy-start.7
  377.7 1.0 copy-done.7
  378.7 3.7 convolution_convert_fusion.1
  382.4 0.0 all-reduce.6.cloned.1.call-update
  382.4 0.8 broadcast_in_dim.32.prior_ref
  383.3 39.1 %shard_map.78 = f32[3,512,4096]{2,1,0:T(8,128)} custom-call(s32[2]{0:T(128)} %pad_add_fusion.at_ref, bf16[5,1024,4096]{2,1,0:T(8,128)(2,1)} %shard_map.77.left_ref.full_ref, f32[6,1024]{1,0:T(8,128)} %stack.15.weight_ref, f32[512,128]{1,0:T(8,128)} %broadcast_in_dim.32.prior_ref, bf16[5,1024,4096]{2,1,0:T(8,128)(2,1)} %shard_map.77.left_ref.full_ref), custom_call_target="tpu_custom_call" | custom-call | flops 21474836480 | bytes 67108864 | tf_op jit(solution)/shard_map/pallas_call | solution.py:415
  422.4 10.9 %all-reduce.6.cloned.1.call-done = bf16[512,2048]{1,0:T(8,128)(2,1)} async-done(((bf16[512,2048]{1,0:T(8,128)(2,1)}), bf16[512,2048]{1,0:T(8,128)(2,1)}) %all-reduce.6.cloned.1.call-update) | async-done | bytes 2097168 | tf_op jit(solution)/shard_map/psum | solution.py:470
  433.3 2.0 multiply_convert_fusion
  435.3 10.0 %fusion.2 = f32[512,4096]{1,0:T(8,128)} fusion(bf16[5,1024,4096]{2,1,0:T(8,128)(2,1)} %shard_map.77.left_ref.full_ref, bf16[512,2048]{1,0:T(8,128)(2,1)S(1)} %multiply_convert_fusion), kind=kOutput, calls=%fused_computation.3 | convolution fusion | flops 4294967296 | bytes 17825792 | tf_op jit(solution)/shard_map/dot_general | solution.py:479
  445.4 10.7 %fusion.1 = bf16[512,4096]{1,0:T(8,128)(2,1)S(1)} fusion(f32[3,512,4096]{2,1,0:T(8,128)} %shard_map.78, f32[512,4096]{1,0:T(8,128)} %fusion.2, bf16[5,1024,4096]{2,1,0:T(8,128)(2,1)} %shard_map.77.left_ref.full_ref, bf16[512,2048]{1,0:T(8,128)(2,1)S(1)} %multiply_convert_fusion), kind=kOutput, calls=%fused_computation.2 | convolution fusion | flops 4301258752 | bytes 30408704 | tf_op jit(solution)/shard_map/dot_general | solution.py:478
  456.1 2.0 copy-done.2
  458.1 1.6 fusion.34
  459.7 2.5 collective-permute-start
  462.2 2.3 collective-permute-start.1
  464.5 2.3 collective-permute-start.2
  466.8 7.4 %collective-permute-done = bf16[512,1024]{1,0:T(8,128)(2,1)S(1)} collective-permute-done((bf16[512,1024]{1,0:T(8,128)(2,1)}, bf16[512,1024]{1,0:T(8,128)(2,1)S(1)}, u32[]{:S(2)}, u32[]{:S(2)}) %collective-permute-start) | collective-permute-done | bytes 1048608 | tf_op jit(solution)/shard_map/ppermute | solution.py:484
  474.2 11.2 %collective-permute-done.1 = bf16[512,1024]{1,0:T(8,128)(2,1)} collective-permute-done((bf16[512,1024]{1,0:T(8,128)(2,1)}, bf16[512,1024]{1,0:T(8,128)(2,1)}, u32[]{:S(2)}, u32[]{:S(2)}) %collective-permute-start.1) | collective-permute-done | bytes 1048608 | tf_op jit(solution)/shard_map/ppermute | solution.py:484
  485.4 2.8 fusion.22
  (18 shorter events, 0.1 us)
Async XLA Ops:
  7.2 30.9 %copy-start = (bf16[1024,512]{1,0:T(8,128)(2,1)S(1)}, bf16[1024,512]{1,0:T(8,128)(2,1)}, u32[]{:S(2)}) copy-start(bf16[1024,512]{1,0:T(8,128)(2,1)} %param.9) | copy-start | bytes 3145732
  7.2 365.7 %all-reduce.4.cloned.1.call-start = ((), (), s32[]{:S(2)}) async-start(), calls=%async_computation | async-start | bytes 8388608 | tf_op jit(solution)/shard_map/psum | solution.py:463
  42.5 390.8 %all-reduce.6.cloned.1.call-start = ((), (), s32[]{:S(2)}) async-start(), calls=%async_computation.1 | async-start | bytes 4194304 | tf_op jit(solution)/shard_map/psum | solution.py:470
  42.6 324.9 %copy-start.3 = (f32[1,1024]{1,0:T(1,128)S(1)}, f32[1,1024]{1,0:T(1,128)}, u32[]{:S(2)}) copy-start(f32[1,1024]{1,0:T(1,128)} %param.7) | copy-start | bytes 12292
  42.6 324.9 %copy-start.4 = (s32[1,1024]{1,0:T(1,128)S(1)}, s32[1,1024]{1,0:T(1,128)}, u32[]{:S(2)}) copy-start(s32[1,1024]{1,0:T(1,128)} %param.6) | copy-start | bytes 12292
  42.6 330.3 %slice-start = ((bf16[4,1024,512]{2,1,0:T(8,128)(2,1)}), bf16[2,1024,512]{2,1,0:T(8,128)(2,1)S(1)}, s32[]{:S(2)}) async-start(bf16[4,1024,512]{2,1,0:T(8,128)(2,1)} %shard_map.76), calls=%async_computation.2 | async-start | bytes 4194304 | tf_op jit(solution)/shard_map/slice | solution.py:467
  372.9 5.8 %copy-start.6 = (bf16[2048,1024]{1,0:T(8,128)(2,1)S(1)}, bf16[2048,1024]{1,0:T(8,128)(2,1)}, u32[]{:S(2)}) copy-start(bf16[2048,1024]{1,0:T(8,128)(2,1)} %all-reduce.4.cloned.1.call-done) | copy-start | bytes 12582916
  377.7 1.0 copy-start.7
  378.7 3.7 copy-start.5
  456.1 2.0 copy-start.2
  458.1 30.1 %copy-start.1 = (bf16[1024,512]{1,0:T(8,128)(2,1)S(1)}, bf16[1024,512]{1,0:T(8,128)(2,1)}, u32[]{:S(2)}) copy-start(bf16[1024,512]{1,0:T(8,128)(2,1)} %param.9) | copy-start | bytes 3145732
  459.7 14.5 %collective-permute-start = (bf16[512,1024]{1,0:T(8,128)(2,1)}, bf16[512,1024]{1,0:T(8,128)(2,1)S(1)}, u32[]{:S(2)}, u32[]{:S(2)}) collective-permute-start(bf16[512,1024]{1,0:T(8,128)(2,1)} %get-tuple-element.7), channel_id=1, source_target_pairs={{8,24},{9,25},{10,26},{11,27},{12,28},{13,29},{14,30},{15,31}} | collective-permute-start | bytes 3145736 | tf_op jit(solution)/shard_map/ppermute | solution.py:484
  462.2 23.2 %collective-permute-start.1 = (bf16[512,1024]{1,0:T(8,128)(2,1)}, bf16[512,1024]{1,0:T(8,128)(2,1)}, u32[]{:S(2)}, u32[]{:S(2)}) collective-permute-start(bf16[512,1024]{1,0:T(8,128)(2,1)} %get-tuple-element.6), channel_id=1, source_target_pairs={{8,16},{9,17},{10,18},{11,19},{12,20},{13,21},{14,22},{15,23}} | collective-permute-start | bytes 3145736 | tf_op jit(solution)/shard_map/ppermute | solution.py:484
  464.5 20.9 %collective-permute-start.2 = (bf16[512,1024]{1,0:T(8,128)(2,1)S(1)}, bf16[512,1024]{1,0:T(8,128)(2,1)}, u32[]{:S(2)}, u32[]{:S(2)}) collective-permute-start(bf16[512,1024]{1,0:T(8,128)(2,1)S(1)} %get-tuple-element.5), channel_id=1, source_target_pairs={{8,0},{9,1},{10,2},{11,3},{12,4},{13,5},{14,6},{15,7}} | collective-permute-start | bytes 3145736 | tf_op jit(solution)/shard_map/ppermute | solution.py:484
Sparse Core Ops, SparseCore 0:
  42.7 240.0 all-reduce.3
  382.5 50.7 all-reduce.5
where the time goes:
time: 497 us; the launch traced here: 495 us
  Pallas kernels  393 us (79%)
  matrix products  33.7 us (7%)
  waiting for transfers between devices  29.5 us (6%)
  between operations  14.2 us (3%)
  local copies, waits for them, and re-layouts  7.83 us (2%)
  starting transfers between devices  7.16 us (1%)
  other arithmetic  5.47 us (1%)
    pallas_call x1, Pallas kernels, gather(): pl.pallas_call(functools.partial(gather_kernel, n_row, n_col), out_shape=...  325 us
    pallas_call x1, Pallas kernels, bands(): pl.pallas_call(bands_kernel, out_shape=jax.ShapeDtypeStruct((3, width, re...  39.1 us
    pallas_call x1, Pallas kernels, exchange(): pl.pallas_call(exchange_kernel, out_shape=jax.ShapeDtypeStruct((4, length...  29.1 us
    ppermute x3, waiting for transfers between devices, body(): moved = lax.ppermute(out[:, w * quarter:(w + 1) * quarter], WEEK, [(1, w)])  18.6 us
    psum x1, waiting for transfers between devices, body(): inner = lax.psum(inner, WEEK)  10.9 us
    dot_general x1, matrix products, body(): jnp.dot(right[:, :length], full[0], preferred_element_type=jnp.float32)  10.7 us
    dot_general x1, matrix products, body(): jnp.dot(right[:, length:], full[1], preferred_element_type=jnp.float32)  10 us
  transfers between devices with their start and end apart: 5, of which 3 were waited for; matrix products, arithmetic and copies ran while one was open for 0% of the time, Pallas kernels for 74%

commit v1 on v0

--- a/solution.py
+++ b/solution.py
@@ -38,8 +38,16 @@
     return out
 
 
-def gather_kernel(n_row, n_col, x_ref, f_ref, own, put_sem, first_s, first_r, main_s, main_r, band_s, band_r,
-                  side_s, side_r, rest_s, rest_r, pass_s, pass_r, flow_s, flow_r):
+def contract_last(left, right):
+    return lax.dot_general(left, right, (((1,), (1,)), ((), ())), preferred_element_type=jnp.float32)
+
+
+def gather_kernel(n_row, n_col, x_ref, pivot_ref, weight_ref, f_ref, panel_ref, inner_ref, weights_ref,
+                  own, put_sem, first_s, first_r, main_s, main_r, band_s, band_r,
+                  side_s, side_r, rest_s, rest_r, pass_s, pass_r, flow_s, flow_r,
+                  low, piv, high, part, came, whole, turned, pan, inn, inn_in, wall,
+                  low_s, low_r, piv_s, piv_r, high_s, high_r, loc, sum_s, sum_r, all_s, all_r,
+                  pan_s, pan_r, inn_s, inn_r, wt_s, wt_r):
     row, col, week = lax.axis_index(ROW), lax.axis_index(COL), lax.axis_index(WEEK)
     _, length, width = x_ref.shape
     half = length // 2
@@ -57,7 +65,13 @@
         pl.semaphore_signal(barrier, inc=1, device_id={COL: lax.rem(col + k, n_col)})
     for k in range(1, n_week):
         pl.semaphore_signal(barrier, inc=1, device_id={WEEK: lax.rem(week + k, n_week)})
-    pl.semaphore_wait(barrier, 2 + (n_col - 1) + (n_week - 1))
+    for k in peers:
+        pl.semaphore_signal(barrier, inc=1, device_id={ROW: n_row - 1 - row, COL: lax.rem(col + k, n_col)})
+    pair = row + 1 - 2 * lax.rem(row, 2)
+    pl.semaphore_signal(barrier, inc=1, device_id={WEEK: n_week - 1 - week, ROW: pair})
+    pl.semaphore_wait(barrier, 2 + 2 * (n_col - 1) + (n_week - 1) + 1)
+    inside = (row > 0) & (row < n_row - 1)
+    outside = (row == 0) | (row == n_row - 1)
 
     slots = [pick(week, UNIT_SLOT[u]) for u in range(UNITS)]
     starts = [pl.multiple_of(pick(week, UNIT_HALF[u]) * half, half) for u in range(UNITS)]
@@ -169,6 +183,297 @@
                 for w in weeks:
                     pl.when(week == w)(functools.partial(body, w))
 
+    far = slab(pair, col)
+    slabs = (mine, far)
+    members = 2 * n_col
+    me = (row - 1) * n_col + col
+    chunk = 2 * length // members
+    slices = pivot_ref.shape[0]
+
+    def op_rows(op):
+        return pl.ds(op * length, length)
+
+    def low_copy(src, j, op, i, device):
+        return remote(src, low_s.at[j, op, i], low_r.at[j, op], device, low.at[j, op_rows(op), :])
+
+    def high_copy(src, j, op, i, device):
+        return remote(src, high_s.at[j, op, i], high_r.at[j, op], device, high.at[j, op_rows(op), :])
+
+    def to_week(w):
+        return {WEEK: jnp.int32(w)}
+
+    def pivot_out():
+        return remote(pivot_ref, piv_s.at[0], piv_r.at[0], {ROW: pair}, piv.at[1])
+
+    def local_copy(src, dst, i):
+        return pltpu.make_async_copy(src, dst, loc.at[i])
+
+    def weight_copy(k):
+        return remote(weight_ref, wt_s.at[k - 1], wt_r.at[k - 1], {WEEK: lax.rem(week + k, n_week)}, wall.at[week])
+
+    ROLES = ((1, 0, 1, 0, 2, 1), (2, 1, 2, 3, 1, 0))
+
+    def early():
+        for k in range(1, n_week):
+            weight_copy(k).start()
+        pltpu.make_async_copy(weight_ref, wall.at[week], wt_s.at[n_week - 1]).start()
+
+        @pl.when(outside)
+        def _():
+            for w, op, lag, *_ in ROLES:
+                @pl.when(week == w)
+                def _(op=op, lag=lag):
+                    low_copy(x_ref.at[lag], 1, op, 0, {ROW: pair}).start()
+            pivot_out().start()
+
+        @pl.when(inside)
+        def _():
+            local_copy(pivot_ref, piv.at[0], 0).start()
+            for w, op, lag, near, across, _ in ROLES:
+                @pl.when(week == w)
+                def _(op=op, lag=lag, near=near, across=across):
+                    low_copy(x_ref.at[lag], 0, op, 0, to_week(across)).start()
+                    low_copy(x_ref.at[lag], 0, op, 1, to_week(near)).start()
+                    local_copy(x_ref.at[lag], low.at[0, op_rows(op), :], 1).start()
+
+    def spread_low():
+        for w, op, lag, near, across, theirs in ROLES:
+            @pl.when(week == w)
+            def _(op=op, lag=lag, near=near, across=across, theirs=theirs):
+                ref = low.at[1, op_rows(op), :]
+                low_copy(ref, 1, op, 0, to_week(across)).wait_recv()
+                low_copy(ref, 1, op, 0, to_week(across)).start()
+                low_copy(ref, 1, op, 1, to_week(near)).start()
+                for j in range(2):
+                    ref = low.at[j, op_rows(theirs), :]
+                    low_copy(ref, j, theirs, 0, to_week(near)).wait_recv()
+                    low_copy(ref, j, theirs, 0, to_week(near)).start()
+                local_copy(x_ref.at[lag], low.at[0, op_rows(op), :], 1).wait()
+
+        @pl.when((week == 0) | (week == n_week - 1))
+        def _():
+            for j in range(2):
+                for op in range(2):
+                    low_copy(low.at[j, op_rows(op), :], j, op, 0, to_week(1)).wait_recv()
+
+        pivot_out().wait_recv()
+        local_copy(pivot_ref, piv.at[0], 0).wait()
+
+    def rows_of(m):
+        return pl.ds(pl.multiple_of(m * chunk, chunk), chunk)
+
+    def member(k):
+        m = lax.rem(me + k, members)
+        return m, {ROW: 1 + m // n_col, COL: lax.rem(m, n_col)}
+
+    def sum_copy(k):
+        m, device = member(k)
+        return remote(part.at[rows_of(m), :], sum_s.at[k - 1], sum_r.at[k - 1], device, came.at[k - 1])
+
+    def all_copy(k):
+        _, device = member(k)
+        return remote(whole.at[rows_of(me), :], all_s.at[k - 1], all_r.at[k - 1], device)
+
+    def make_part():
+        @pl.loop(0, members)
+        def _(m):
+            at = rows_of(m)
+            total = contract_last(low[0, at, :], piv[0]) + contract_last(low[1, at, :], piv[1])
+            part[at, :] = total.astype(part.dtype)
+
+        for k in range(1, members):
+            sum_copy(k).start()
+
+    def make_whole():
+        for k in range(1, members):
+            sum_copy(k).wait_recv()
+        total = part[rows_of(me), :].astype(jnp.float32)
+        for k in range(1, members):
+            total = total + came[k - 1].astype(jnp.float32)
+        whole[rows_of(me), :] = total.astype(whole.dtype)
+        for k in range(1, members):
+            all_copy(k).start()
+
+    def column(slot, s):
+        return f_ref.at[slot, :, pl.ds(pl.multiple_of(s * width, width), width)]
+
+    def early_flow(s):
+        ref = cell(0, 0, s)
+        return remote(ref, flow_s.at[0, s], flow_r.at[3, s], {ROW: target[0]})
+
+    def start_high():
+        @pl.when((week == 1) | (week == 2))
+        def _():
+            for s in slabs:
+                early_flow(s).wait_recv()
+
+        @pl.when(week == 1)
+        def _():
+            for j, s in enumerate(slabs):
+                high_copy(column(0, s), j, 0, 0, to_week(2)).start()
+                high_copy(column(0, s), j, 0, 1, to_week(0)).start()
+                high_copy(column(1, s), j, 1, 0, to_week(0)).start()
+                local_copy(column(0, s), high.at[j, op_rows(0), :], 2 + j).start()
+                local_copy(column(1, s), high.at[j, op_rows(1), :], 4 + j).start()
+
+        @pl.when(week == 2)
+        def _():
+            for j, s in enumerate(slabs):
+                high_copy(column(3, s), j, 1, 0, to_week(3)).start()
+                local_copy(column(3, s), high.at[j, op_rows(1), :], 4 + j).start()
+
+    def wait_high():
+        for j, s in enumerate(slabs):
+            @pl.when(week == 1)
+            def _(j=j, s=s):
+                local_copy(column(0, s), high.at[j, op_rows(0), :], 2 + j).wait()
+
+            @pl.when(week != 1)
+            def _(j=j):
+                high_copy(high.at[j, op_rows(0), :], j, 0, 0, to_week(3)).wait_recv()
+
+            @pl.when(week == 2)
+            def _(j=j):
+                high_copy(high.at[j, op_rows(0), :], j, 0, 0, to_week(3)).start()
+
+            @pl.when((week == 1) | (week == 2))
+            def _(j=j, s=s):
+                local_copy(column(1, s), high.at[j, op_rows(1), :], 4 + j).wait()
+
+            @pl.when((week == 0) | (week == n_week - 1))
+            def _(j=j):
+                high_copy(high.at[j, op_rows(1), :], j, 1, 0, to_week(3)).wait_recv()
+
+    def panel_out():
+        return remote(pan.at[1], pan_s.at[0], pan_r.at[0], {ROW: pair}, panel_ref)
+
+    def inner_near(j):
+        return remote(inn.at[j], inn_s.at[j], inn_r.at[j], {WEEK: jnp.where(week == 0, 1, 2)}, inn_in.at[j])
+
+    def inner_far(j, i):
+        device = {WEEK: jnp.int32(1)} if j == 0 else {WEEK: jnp.int32(1), ROW: pair}
+        return remote(inn.at[j], inn_s.at[j], inn_r.at[2 + i], device, inner_ref.at[i])
+
+    def make_panel():
+        for k in range(1, members):
+            all_copy(k).wait_recv()
+        wait_high()
+        for k in range(1, n_week):
+            weight_copy(k).wait_recv()
+        pltpu.make_async_copy(weight_ref, wall.at[week], wt_s.at[n_week - 1]).wait()
+        step = min(length, 512)
+        for j in range(2):
+            for op in range(2):
+                for at in range(0, length, step):
+                    rows = pl.ds(op * length + at, step)
+                    flat = high[j, rows, :].T.astype(jnp.float32) * wall[1 + op, 1 + op, pl.ds(at, step)][None, :]
+                    turned[j, :, rows] = flat.astype(turned.dtype)
+        tile = min(slices, 256)
+        for j in range(2):
+            @pl.loop(0, slices // tile)
+            def _(i, j=j):
+                at = pl.ds(pl.multiple_of(i * tile, tile), tile)
+                pan[j, :, at] = jnp.dot(turned[j], whole[:, at], preferred_element_type=jnp.float32).astype(pan.dtype)
+
+            if j == 0:
+                local_copy(pan.at[0], panel_ref, 0).start()
+            else:
+                panel_out().start()
+        for j in (1, 0):
+            @pl.loop(0, 2 * length // tile)
+            def _(i, j=j):
+                at = pl.ds(pl.multiple_of(i * tile, tile), tile)
+                inn[j, :, at] = contract_last(pan[j], whole[at, :]).astype(inn.dtype)
+
+            @pl.when((week == 0) | (week == n_week - 1))
+            def _(j=j):
+                inner_near(j).start()
+
+    def join_inner():
+        @pl.when((week == 1) | (week == 2))
+        def _():
+            for j in (1, 0):
+                inner_near(j).wait_recv()
+                inn[j] = (inn[j].astype(jnp.float32) + inn_in[j].astype(jnp.float32)).astype(inn.dtype)
+
+                @pl.when(week == 2)
+                def _(j=j):
+                    inner_far(j, 1).start()
+
+                @pl.when(week == 1)
+                def _(j=j):
+                    if j == 1:
+                        inner_far(1, 0).start()
+                    else:
+                        local_copy(inn.at[0], inner_ref.at[0], 1).start()
+
+    def end_inner():
+        @pl.when(week == 1)
+        def _():
+            inner_far(1, 1).wait_recv()
+            pl.when(outside)(lambda: inner_far(1, 0).wait_recv())
+
+        @pl.when(outside)
+        def _():
+            panel_out().wait_recv()
+            for k in range(1, n_week):
+                weight_copy(k).wait_recv()
+            pltpu.make_async_copy(weight_ref, wall.at[week], wt_s.at[n_week - 1]).wait()
+            for w, op, lag, *_ in ROLES:
+                @pl.when(week == w)
+                def _(op=op, lag=lag):
+                    low_copy(x_ref.at[lag], 1, op, 0, {ROW: pair}).wait_send()
+            pivot_out().wait_send()
+
+        for k in range(1, n_week):
+            weight_copy(k).wait_send()
+
+        @pl.when(inside)
+        def _():
+            for w, op, lag, near, across, theirs in ROLES:
+                @pl.when(week == w)
+                def _(op=op, theirs=theirs):
+                    for j in range(2):
+                        for i in range(2):
+                            low_copy(x_ref.at[0], j, op, i, to_week(0)).wait_send()
+                        low_copy(x_ref.at[0], j, theirs, 0, to_week(0)).wait_send()
+            for k in range(1, members):
+                sum_copy(k).wait_send()
+                all_copy(k).wait_send()
+
+            @pl.when(week == 1)
+            def _():
+                for j, s in enumerate(slabs):
+                    high_copy(column(0, s), j, 0, 0, to_week(2)).wait_send()
+                    high_copy(column(0, s), j, 0, 1, to_week(0)).wait_send()
+                    high_copy(column(1, s), j, 1, 0, to_week(0)).wait_send()
+
+            @pl.when(week == 2)
+            def _():
+                for j, s in enumerate(slabs):
+                    high_copy(column(3, s), j, 1, 0, to_week(3)).wait_send()
+                    high_copy(high.at[j, op_rows(0), :], j, 0, 0, to_week(3)).wait_send()
+
+            local_copy(pan.at[0], panel_ref, 0).wait()
+            panel_out().wait_send()
+            for j in range(2):
+                @pl.when((week == 0) | (week == n_week - 1))
+                def _(j=j):
+                    inner_near(j).wait_send()
+
+                @pl.when(week == 2)
+                def _(j=j):
+                    inner_far(j, 1).wait_send()
+
+            @pl.when(week == 1)
+            def _():
+                inner_far(1, 0).wait_send()
+                local_copy(inn.at[0], inner_ref.at[0], 1).wait()
+
+        pltpu.make_async_copy(wall, weights_ref, wt_s.at[n_week - 1]).start()
+        pltpu.make_async_copy(wall, weights_ref, wt_s.at[n_week - 1]).wait()
+
+    early()
     first("start")
     for u in range(UNITS):
         local(u, lambda w, u=u: take(u, w).start())
@@ -209,6 +514,11 @@
                     pl.when(has[d])(lambda d=d, k=k: strip(u, 0, d, k).start())
 
         active(u, spread_band)
+
+    @pl.when(inside)
+    def _():
+        spread_low()
+        make_part()
 
     def across(step):
         for u in range(UNITS):
@@ -260,6 +570,15 @@
         across(step - 1)
         if step > 1:
             relays(step - 2, "start")
+        if step == 1:
+            @pl.when(inside)
+            def _():
+                make_whole()
+                start_high()
+        if step == n_row - 2:
+            pl.when(inside)(make_panel)
+        if step == n_row - 1:
+            pl.when(inside)(join_inner)
     across(n_row - 1)
     for step in range(max(n_row - 2, 0), n_row):
         relays(step, "start")
@@ -268,9 +587,16 @@
     def _():
         for s in range(n):
             for flow in range(FLOWS):
-                ref = cell(0, 0, s)
-                remote(ref, flow_s.at[0, s], flow_r.at[flow, s], {ROW: target[0]}).wait_recv()
-
+                def arrive(s=s, flow=flow):
+                    ref = cell(0, 0, s)
+                    remote(ref, flow_s.at[0, s], flow_r.at[flow, s], {ROW: target[0]}).wait_recv()
+
+                if flow == 3:
+                    pl.when(outside | ((mine != s) & (far != s)))(arrive)
+                else:
+                    arrive()
+
+    end_inner()
     first("wait")
     for u in range(UNITS):
         def finish(u=u):
@@ -303,80 +629,45 @@
         relay(s, "wait")
 
 
-def gather(x, collective_id):
+def gather(x, pivot, weight, collective_id):
     n_row, n_col = lax.axis_size(ROW), lax.axis_size(COL)
     _, length, width = x.shape
+    slices = pivot.shape[0]
     n = n_row * n_col
+    assert n_row == 4 and lax.axis_size(WEEK) == 4
     kinds = (UNITS, n_row - 1, 2)
     wide = (*kinds, n_col - 1)
     sides = (UNITS, n_col - 1)
+    members = 2 * n_col
+    vmem = functools.partial(lambda *shape: pltpu.VMEM(shape, x.dtype))
     sent = length * width * 2 * (n - 1) * 9 // 4
+    hbm = pl.BlockSpec(memory_space=pl.ANY)
     return pl.pallas_call(
         functools.partial(gather_kernel, n_row, n_col),
-        out_shape=jax.ShapeDtypeStruct((5, length, width * n), x.dtype),
-        in_specs=[pl.BlockSpec(memory_space=pl.ANY)],
-        out_specs=pl.BlockSpec(memory_space=pl.ANY),
+        out_shape=(
+            jax.ShapeDtypeStruct((5, length, width * n), x.dtype),
+            jax.ShapeDtypeStruct((width, slices), x.dtype),
+            jax.ShapeDtypeStruct((2, width, 2 * length), x.dtype),
+            jax.ShapeDtypeStruct((4, *weight.shape), weight.dtype),
+        ),
+        in_specs=[hbm] * 3,
+        out_specs=(hbm,) * 4,
         scratch_shapes=[
             pltpu.VMEM((UNITS, length // 2, width), x.dtype), DMA((UNITS,)), DMA((UNITS,)), DMA((UNITS,)),
             DMA(kinds), DMA(kinds), DMA(wide), DMA(wide), DMA(sides), DMA(sides), DMA(sides), DMA(sides),
             DMA(wide), DMA(wide), DMA((5, n)), DMA((FLOWS, n)),
+            vmem(2, 2 * length, width), vmem(2, slices, width), vmem(2, 2 * length, width),
+            vmem(2 * length, slices), vmem(members - 1, 2 * length // members, slices), vmem(2 * length, slices),
+            vmem(2, width, 2 * length), vmem(2, width, slices), vmem(2, width, 2 * length),
+            vmem(2, width, 2 * length), pltpu.VMEM((4, *weight.shape), weight.dtype),
+            DMA((2, 2, 2)), DMA((2, 2)), DMA((1,)), DMA((1,)), DMA((2, 2, 2)), DMA((2, 2)), DMA((6,)),
+            DMA((members - 1,)), DMA((members - 1,)), DMA((members - 1,)), DMA((members - 1,)),
+            DMA((1,)), DMA((1,)), DMA((2,)), DMA((4,)), DMA((4,)), DMA((3,)),
         ],
-        compiler_params=pltpu.CompilerParams(collective_id=collective_id, has_side_effects=True),
+        compiler_params=pltpu.CompilerParams(
+            collective_id=collective_id, has_side_effects=True, vmem_limit_bytes=60 << 20),
         cost_estimate=pl.CostEstimate(flops=0, bytes_accessed=sent * 8, transcendentals=0),
-    )(x)
-
-
-def exchange_kernel(x_ref, e_ref, own, put_sem, send, recv):
-    week = lax.axis_index(WEEK)
-    n_week = 4
-    barrier = pltpu.get_barrier_semaphore()
-    for k in range(1, n_week):
-        pl.semaphore_signal(barrier, inc=1, device_id={WEEK: lax.rem(week + k, n_week)})
-    pl.semaphore_wait(barrier, n_week - 1)
-    roles = ((1, ((1, 2), (0, 0)), 0, 2), (2, ((2, 3), (1, 1)), 3, 1))
-
-    def copy(src, place, to, sem):
-        return pltpu.make_async_remote_copy(src, e_ref.at[place], send.at[place, sem], recv.at[place],
-                                            device_id={WEEK: jnp.int32(to)})
-
-    for w, items, near, far in roles:
-        @pl.when(week == w)
-        def _(w=w, items=items, near=near, far=far):
-            for lag, at in items:
-                copy(x_ref.at[lag], at, far, 0).start()
-            for lag, at in items:
-                copy(x_ref.at[lag], at, near, 1).start()
-                pltpu.make_async_copy(x_ref.at[lag], own.at[lag], put_sem.at[lag]).start()
-            for lag, at in items:
-                pltpu.make_async_copy(x_ref.at[lag], own.at[lag], put_sem.at[lag]).wait()
-                pltpu.make_async_copy(own.at[lag], e_ref.at[at], put_sem.at[lag]).start()
-            theirs = roles[2 - w][1]
-            for _, at in theirs:
-                copy(e_ref.at[at], at, near, 0).wait_recv()
-                copy(e_ref.at[at], at, near, 0).start()
-            for lag, at in items:
-                copy(x_ref.at[lag], at, far, 0).wait_send()
-                copy(x_ref.at[lag], at, near, 1).wait_send()
-                pltpu.make_async_copy(own.at[lag], e_ref.at[at], put_sem.at[lag]).wait()
-            for _, at in theirs:
-                copy(e_ref.at[at], at, near, 0).wait_send()
-
-    @pl.when((week == 0) | (week == n_week - 1))
-    def _():
-        for at in range(4):
-            copy(e_ref.at[at], at, 0, 0).wait_recv()
-
-
-def exchange(x, collective_id):
-    _, length, width = x.shape
-    return pl.pallas_call(
-        exchange_kernel,
-        out_shape=jax.ShapeDtypeStruct((4, length, width), x.dtype),
-        in_specs=[pl.BlockSpec(memory_space=pl.ANY)],
-        out_specs=pl.BlockSpec(memory_space=pl.ANY),
-        scratch_shapes=[pltpu.VMEM(x.shape, x.dtype), DMA((3,)), DMA((4, 2)), DMA((4,))],
-        compiler_params=pltpu.CompilerParams(collective_id=collective_id, has_side_effects=True),
-    )(x)
+    )(x, pivot, weight)
 
 
 PRODUCTS = ((0, 0, 0, (0, 3)), (0, 1, 1, (0, 2)), (0, 2, 2, (0, 1)), (1, 0, 3, (1, 3)), (1, 1, 4, (1, 2)),
@@ -434,55 +725,84 @@
     )(at, full, weights, prior, full)
 
 
-def contract_first(left, right):
-    return lax.dot_general(left, right, (((0,), (0,)), ((), ())), preferred_element_type=jnp.float32)
-
-
-def contract_last(left, right):
-    return lax.dot_general(left, right, (((1,), (1,)), ((), ())), preferred_element_type=jnp.float32)
+def schur_kernel(at_ref, left_ref, weight_ref, prior_ref, inner_ref, full_ref, out_ref, turned):
+    week, mine = at_ref[0], at_ref[1]
+    tile = pl.program_id(0)
+    slots, length, width = left_ref.shape
+    columns = full_ref.shape[2]
+
+    @pl.when(week == 1)
+    def _():
+        @pl.when(tile == 0)
+        def _():
+            for k in range(slots):
+                flat = left_ref[k].T.astype(jnp.float32) * weight_ref[k][None, :]
+                if k < 2:
+                    at = pl.ds(k * length, length)
+                    inner = inner_ref[0, :, at].astype(jnp.float32) + inner_ref[1, :, at].astype(jnp.float32)
+                    flat = flat - inner * weight_ref[3 + k][None, :]
+                turned[k] = flat.astype(turned.dtype)
+
+        total = jnp.dot(turned[0], full_ref[0], preferred_element_type=jnp.float32)
+        for k in range(1, slots):
+            total = total + jnp.dot(turned[k], full_ref[k], preferred_element_type=jnp.float32)
+        row_ids = lax.broadcasted_iota(jnp.int32, (width, columns), 0) + mine * width
+        col_ids = lax.broadcasted_iota(jnp.int32, (width, columns), 1) + tile * columns
+        total = total + jnp.where(row_ids == col_ids, prior_ref[:, :1], 0.0)
+        out_ref[...] = total.astype(out_ref.dtype)
+
+
+def schur_rows(at, full, weights, prior, inner):
+    _, length, regions = full.shape
+    width = prior.shape[0]
+    columns = min(512, regions)
+    whole = pl.Buffered(1)
+    return pl.pallas_call(
+        schur_kernel,
+        out_shape=jax.ShapeDtypeStruct((width, regions), jnp.bfloat16),
+        grid_spec=pltpu.PrefetchScalarGridSpec(
+            num_scalar_prefetch=1,
+            grid=(regions // columns,),
+            in_specs=[
+                pl.BlockSpec((3, length, width), lambda j, at: (0, 0, at[1]), pipeline_mode=whole),
+                pl.BlockSpec(weights.shape, lambda j, at: (0, 0)),
+                pl.BlockSpec(prior.shape, lambda j, at: (0, 0)),
+                pl.BlockSpec(inner.shape, lambda j, at: (0, 0, 0), pipeline_mode=whole),
+                pl.BlockSpec((3, length, columns), lambda j, at: (0, 0, jnp.where(at[0] == 1, j, 0))),
+            ],
+            out_specs=pl.BlockSpec((width, columns), lambda j, at: (0, j)),
+            scratch_shapes=[pltpu.VMEM((3, width, length), full.dtype)],
+        ),
+        compiler_params=pltpu.CompilerParams(dimension_semantics=("arbitrary",), vmem_limit_bytes=60 << 20),
+        cost_estimate=pl.CostEstimate(
+            flops=6 * width * length * regions, bytes_accessed=6 * length * regions, transcendentals=0),
+    )(at, full, weights, prior, inner, full)
 
 
 def body(sensitivity, reach, obs_weight, prior_precision, pivot_solve):
     week = lax.axis_index(WEEK)
-    n_week, n_row, n_col = (lax.axis_size(name) for name in (WEEK, ROW, COL))
-    assert n_week == 4
+    n_week, n_col = lax.axis_size(WEEK), lax.axis_size(COL)
     local = sensitivity[0]
     lags, length, width = local.shape
     mine = lax.axis_index(ROW) * n_col + lax.axis_index(COL)
 
-    lag = jnp.arange(lags)[:, None]
-    own_weight = jnp.where((reach >= lag) & (week >= lag), obs_weight, 0.0)
-    by_week = lax.all_gather(own_weight, WEEK)
+    lag = jnp.arange(8)[:, None]
+    own_weight = jnp.where((reach >= lag) & (week >= lag) & (lag < lags), obs_weight, 0.0)
+    full, panel, inner, by_week = gather(local, pivot_solve, own_weight, 0)
+    by_week = by_week[:, :lags]
     later = jnp.concatenate([by_week, jnp.zeros((lags, lags, length), by_week.dtype)])
     here = lax.dynamic_slice(later, (week, 0, 0), (lags, lags, length))
     weights = jnp.stack([here[0, 0], here[1, 1], here[2, 2], here[0, 1], here[1, 2], here[0, 2]])
 
-    near = exchange(local, 1)
-    low = jnp.concatenate([near[2], near[3]])
-    part = contract_last(low, pivot_solve).astype(jnp.bfloat16)
-    whole = lax.psum(part, (ROW, COL))
-    part, local = lax.optimization_barrier((part, local))
-    full = gather(local, 0)
-    panel_weight = jnp.concatenate([by_week[1, 1], by_week[2, 2]])
-    left = (panel_weight[:, None] * near[:2].reshape(2 * length, width).astype(jnp.float32)).astype(jnp.bfloat16)
-    panel = contract_first(left, whole).astype(jnp.bfloat16)
-    inner = contract_last(panel, whole).astype(jnp.bfloat16)
-    inner = lax.psum(inner, WEEK)
-
     at = jnp.stack([week, mine]).astype(jnp.int32)
     prior = jnp.broadcast_to(prior_precision[0][:, None], (width, 128))
-    h = bands(at, full, weights, prior)
-
-    right = (inner.astype(jnp.float32) * panel_weight).astype(jnp.bfloat16)
-    spent = right.shape[0]
-    out = h[0] - (jnp.dot(right[:, :length], full[0], preferred_element_type=jnp.float32)
-                  + jnp.dot(right[:, length:], full[1], preferred_element_type=jnp.float32))
-    out = out.astype(jnp.bfloat16)
+    out = schur_rows(at, full, weights, prior, inner)
     quarter = out.shape[1] // n_week
     schur = out[:, quarter : 2 * quarter]
-    for w in (0, 2, 3):
-        moved = lax.ppermute(out[:, w * quarter : (w + 1) * quarter], WEEK, [(1, w)])
-        schur = jnp.where(week == w, moved, schur)
+    moved = [(w, lax.ppermute(out[:, w * quarter : (w + 1) * quarter], WEEK, [(1, w)])) for w in (2, 3, 0)]
+    h = bands(at, full, weights, prior)
+    for w, block in moved:
+        schur = jnp.where(week == w, block, schur)
     return (h[None], panel, schur.astype(jnp.float32))
 
 

time: 497 us -> 398 us (0.80)
  the two profiles are of different devices: /device:TPU:5 before, /device:TPU:17 now
where the time goes in v1:
time: 398 us; the launch traced here: 397 us
  Pallas kernels  380 us (95%)
  local copies, waits for them, and re-layouts  6.9 us (2%)
  starting transfers between devices  4.97 us (1%)
  other arithmetic  4.88 us (1%)
    pallas_call x1, Pallas kernels, gather(): pl.pallas_call(functools.partial(gather_kernel, n_row, n_col), out_shape=...  318 us
    pallas_call x1, Pallas kernels, bands(): pl.pallas_call(bands_kernel, out_shape=jax.ShapeDtypeStruct((3, width, re...  39 us
    pallas_call x1, Pallas kernels, schur_rows(): pl.pallas_call(schur_kernel, out_shape=jax.ShapeDtypeStruct((width, regio...  22.8 us
  transfers between devices with their start and end apart: 3, of which 0 were waited for; matrix products, arithmetic and copies ran while one was open for 0% of the time, Pallas kernels for 10%

profile of v1, /device:TPU:17, one launch (start us, length us, event | category | flops | bytes accessed | tf_op | source)
XLA Modules:
  0.0 397.0 jit_solution(12330129145560900104)
XLA Ops:
  0.6 0.0 copy-start.1
  0.7 1.4 fusion.5.weight_ref
  2.1 317.9 %shard_map.76 = (bf16[5,1024,4096]{2,1,0:T(8,128)(2,1)}, bf16[512,1024]{1,0:T(8,128)(2,1)}, bf16[2,512,2048]{2,1,0:T(8,128)(2,1)}, f32[4,8,1024]{2,1,0:T(8,128)}) custom-call(bf16[3,1024,512]{2,1,0:T(8,128)(2,1)} %bitcast.20, bf16[1024,512]{1,0:T(8,128)(2,1)} %pivot_ref.1, f32[8,1024]{1,0:T(8,128)} %fusion.5.weight_ref), custom_call_target="tpu_custom_call" | custom-call | bytes 132120576 | tf_op jit(solution)/shard_map/pallas_call | solution.py:645
  319.9 0.9 slice.33
  320.8 0.6 pad_add_fusion.at_ref
  321.5 0.7 stack.15.weight_ref
  322.2 0.0 copy-done.1
  322.2 0.8 broadcast_in_dim.30.prior_ref
  323.0 22.8 %shard_map.78 = bf16[512,4096]{1,0:T(8,128)(2,1)} custom-call(s32[2]{0:T(128)} %pad_add_fusion.at_ref, bf16[5,1024,4096]{2,1,0:T(8,128)(2,1)} %get-tuple-element.7.left_ref.full_ref, f32[6,1024]{1,0:T(8,128)} %stack.15.weight_ref, f32[512,128]{1,0:T(8,128)} %broadcast_in_dim.30.prior_ref, bf16[2,512,2048]{2,1,0:T(8,128)(2,1)} %get-tuple-element.10.inner_ref, ...), custom_call_target="tpu_custom_call" | custom-call | flops 12884901888 | bytes 25165824 | tf_op jit(solution)/shard_map/pallas_call | solution.py:760
  345.8 3.5 fusion.12
  349.2 1.3 collective-permute-start
  350.6 1.4 collective-permute-start.1
  352.0 2.3 collective-permute-start.2
  354.2 39.0 %shard_map.77 = f32[3,512,4096]{2,1,0:T(8,128)} custom-call(s32[2]{0:T(128)} %pad_add_fusion.at_ref, bf16[5,1024,4096]{2,1,0:T(8,128)(2,1)} %get-tuple-element.7.left_ref.full_ref, f32[6,1024]{1,0:T(8,128)} %stack.15.weight_ref, f32[512,128]{1,0:T(8,128)} %broadcast_in_dim.30.prior_ref, bf16[5,1024,4096]{2,1,0:T(8,128)(2,1)} %get-tuple-element.7.left_ref.full_ref), custom_call_target="tpu_custom_call" | custom-call | flops 21474836480 | bytes 67108864 | tf_op jit(solution)/shard_map/pallas_call | solution.py:706
  393.2 0.0 copy-start
  393.2 0.0 collective-permute-done
  393.2 0.0 collective-permute-done.1
  393.2 0.0 collective-permute-done.2
  393.2 2.9 fusion.2
  396.1 0.0 copy-done
  396.1 1.0 copy.9
  (2 shorter events, 0.0 us)
Async XLA Ops:
  0.6 321.5 %copy-start.1 = (f32[1,512]{1,0:T(1,128)S(1)}, f32[1,512]{1,0:T(1,128)}, u32[]{:S(2)}) copy-start(f32[1,512]{1,0:T(1,128)} %param.8) | copy-start | bytes 6148
  349.2 43.9 %collective-permute-start = (bf16[512,1024]{1,0:T(8,128)(2,1)}, bf16[512,1024]{1,0:T(8,128)(2,1)S(1)}, u32[]{:S(2)}, u32[]{:S(2)}) collective-permute-start(bf16[512,1024]{1,0:T(8,128)(2,1)} %get-tuple-element.13), channel_id=1, source_target_pairs={{8,0},{9,1},{10,2},{11,3},{12,4},{13,5},{14,6},{15,7}} | collective-permute-start | bytes 3145736 | tf_op jit(solution)/shard_map/ppermute | solution.py:802
  350.6 42.6 %collective-permute-start.1 = (bf16[512,1024]{1,0:T(8,128)(2,1)}, bf16[512,1024]{1,0:T(8,128)(2,1)S(1)}, u32[]{:S(2)}, u32[]{:S(2)}) collective-permute-start(bf16[512,1024]{1,0:T(8,128)(2,1)} %get-tuple-element.12), channel_id=1, source_target_pairs={{8,24},{9,25},{10,26},{11,27},{12,28},{13,29},{14,30},{15,31}} | collective-permute-start | bytes 3145736 | tf_op jit(solution)/shard_map/ppermute | solution.py:802
  352.0 41.2 %collective-permute-start.2 = (bf16[512,1024]{1,0:T(8,128)(2,1)S(1)}, bf16[512,1024]{1,0:T(8,128)(2,1)}, u32[]{:S(2)}, u32[]{:S(2)}) collective-permute-start(bf16[512,1024]{1,0:T(8,128)(2,1)S(1)} %get-tuple-element.11), channel_id=1, source_target_pairs={{8,16},{9,17},{10,18},{11,19},{12,20},{13,21},{14,22},{15,23}} | collective-permute-start | bytes 3145736 | tf_op jit(solution)/shard_map/ppermute | solution.py:802
  393.2 2.9 copy-start

commit v2 on v1

v2 whole, which is shorter than its diff:
```python
import functools

import jax
import jax.numpy as jnp
from jax import lax
from jax.experimental import pallas as pl
from jax.experimental.pallas import tpu as pltpu
from jax.sharding import PartitionSpec as P

ROW, COL, WEEK = "row", "col", "week"
DMA = pltpu.SemaphoreType.DMA

UNITS = 5
UNIT_SLOT = ((0, 0, 0, 0), (0, 0, 0, 0), (1, 1, 3, 3), (1, 2, 2, 3), (2, 0, 0, 2))
UNIT_HALF = ((0, 0, 0, 0), (1, 1, 1, 1), (0, 0, 1, 0), (1, 0, 1, 1), (0, 0, 0, 1))
LOCAL = {
    0: ((0, 0),) * 4,
    1: ((0, 1),) * 4,
    2: (None, None, (1, 1), (1, 0)),
    3: (None, None, (2, 1), (1, 1)),
    4: (None, None, None, (2, 1)),
}
FIRST = ((1, 1, 0, 0, 2), (1, 1, 1, 0, 3), (2, 2, 0, 0, 4), (2, 1, 0, 1, 2), (3, 2, 0, 1, 3))
ONWARD = (
    ((2, 1, 3, 0), (3, 1, 3, 1), (4, 1, 4, 2), (4, 2, 2, 4)),
    ((2, 2, 3, 3), (3, 3, 2, 0)),
    ((2, 1, 1, 3), (3, 0, 2, 0)),
    ((2, 2, 1, 0), (3, 2, 1, 1), (4, 2, 4, 2), (4, 1, 2, 4)),
)
RELAY = {0: (1, 1, 4), 3: (0, 2, 4)}
FLOWS = 6


def pick(week, values):
    out = jnp.int32(values[0])
    for k, value in enumerate(values[1:], 1):
        out = jnp.where(week == k, jnp.int32(value), out)
    return out


def contract_last(left, right):
    return lax.dot_general(left, right, (((1,), (1,)), ((), ())), preferred_element_type=jnp.float32)


def gather_kernel(n_row, n_col, x_ref, pivot_ref, weight_ref, f_ref, panel_ref, inner_ref, weights_ref,
                  own, put_sem, first_s, first_r, z_s, z_r, pair_s, cross_s, cross_r, y_s, y_r, flow_s, flow_r,
                  low, piv, high, part, came_z, came_y, whole, turned, pan, inn, inn_in, wall,
                  low_s, low_r, piv_s, piv_r, high_s, high_r, loc, half_s, half_r, sum_s, sum_r,
                  all_s, all_r, back_s, back_r, pan_s, pan_r, inn_s, inn_r, wt_s, wt_r):
    row, col, week = lax.axis_index(ROW), lax.axis_index(COL), lax.axis_index(WEEK)
    _, length, width = x_ref.shape
    half = length // 2
    n = n_row * n_col
    peers = range(1, n_col)
    n_week = 4
    pair = row + 1 - 2 * lax.rem(row, 2)
    opp = jnp.where(row < 2, 2, 1)
    end = jnp.where(row < 2, 3, 0)
    inside = (row == 1) | (row == 2)
    outside = (row == 0) | (row == 3)
    middle = (week == 1) | (week == 2)
    edge = (week == 0) | (week == n_week - 1)

    barrier = pltpu.get_barrier_semaphore()
    for k in (1, n_row - 1):
        pl.semaphore_signal(barrier, inc=1, device_id={ROW: lax.rem(row + k, n_row)})
    for k in peers:
        pl.semaphore_signal(barrier, inc=1, device_id={COL: lax.rem(col + k, n_col)})
    for k in range(1, n_week):
        pl.semaphore_signal(barrier, inc=1, device_id={WEEK: lax.rem(week + k, n_week)})
    pl.semaphore_signal(barrier, inc=1, device_id={WEEK: n_week - 1 - week, ROW: pair})
    pl.semaphore_wait(barrier, 2 + (n_col - 1) + (n_week - 1) + 1)

    slots = [pick(week, UNIT_SLOT[u]) for u in range(UNITS)]
    starts = [pl.multiple_of(pick(week, UNIT_HALF[u]) * half, half) for u in range(UNITS)]

    def slab(at_row, at_col):
        return at_row * n_col + at_col

    mine, far = slab(row, col), slab(pair, col)

    def cell(slot, start, s):
        at = pl.ds(pl.multiple_of(s * width, width), width)
        return f_ref.at[slot, pl.ds(start, half), at]

    def place(u, s):
        return cell(slots[u], starts[u], s)

    def active(u, body):
        if u < 4:
            body()
        else:
            pl.when(edge)(body)

    def other(k):
        return lax.rem(col + n_col - k, n_col)

    def remote(ref, s_sem, r_sem, device, to=None):
        return pltpu.make_async_remote_copy(ref, ref if to is None else to, s_sem, r_sem, device_id=device)

    def to_pair(u, s, hop):
        return remote(place(u, s), pair_s.at[u, hop], z_r.at[u, hop], {ROW: pair})

    def to_opp(u, s, hop):
        return remote(place(u, s), z_s.at[u, hop], z_r.at[u, hop], {ROW: opp})

    def cross(u, k):
        return remote(place(u, slab(row, other(k))), cross_s.at[u, k - 1], cross_r.at[u, k - 1], {ROW: pair})

    def side(u, s, hop, k):
        return remote(place(u, s), y_s.at[u, hop, k - 1], y_r.at[u, hop, k - 1], {COL: lax.rem(col + k, n_col)})

    def aside(u, s, hop):
        for k in peers:
            side(u, s, hop, k).start()

    def flows(w, u, s):
        for i, (unit, to_week, to_slot, flow) in enumerate(ONWARD[w]):
            if unit == u:
                start = UNIT_HALF[u][w] * half
                yield remote(cell(UNIT_SLOT[u][w], start, s), flow_s.at[i, s], flow_r.at[flow, s],
                             {WEEK: jnp.int32(to_week)}, cell(to_slot, start, s))

    def spread(u, s, act="start"):
        for w in range(n_week):
            if any(unit == u for unit, *_ in ONWARD[w]):
                @pl.when(week == w)
                def _(w=w):
                    for copy in flows(w, u, s):
                        copy.start() if act == "start" else copy.wait_send()

    def relay(s, act="start"):
        for w, (h, to_week, to_slot) in RELAY.items():
            @pl.when(week == w)
            def _(w=w, h=h, to_week=to_week, to_slot=to_slot):
                ref = cell(2, h * half, s)
                copy = remote(ref, flow_s.at[4, s], flow_r.at[5, s], {WEEK: jnp.int32(to_week)},
                              cell(to_slot, h * half, s))
                if act == "start":
                    remote(ref, flow_s.at[0, s], flow_r.at[0, s], {WEEK: jnp.int32(to_week)}).wait_recv()
                    copy.start()
                else:
                    copy.wait_send()

    def relays(at_row):
        relay(slab(at_row, col))
        for k in peers:
            relay(slab(at_row, other(k)))

    def first(act):
        for w, lag, h, to_week, u in FIRST:
            @pl.when(week == w)
            def _(lag=lag, h=h, to_week=to_week, u=u):
                copy = remote(x_ref.at[lag, pl.ds(h * half, half), :], first_s.at[u], first_r.at[u],
                              {WEEK: jnp.int32(to_week)}, cell(UNIT_SLOT[u][to_week], h * half, mine))
                copy.start() if act == "start" else copy.wait_send()

    def take(u, w):
        lag, h = LOCAL[u][w]
        return pltpu.make_async_copy(x_ref.at[lag, pl.ds(h * half, half), :], own.at[u], put_sem.at[u])

    def put(u):
        return pltpu.make_async_copy(own.at[u], place(u, mine), put_sem.at[u])

    def local(u, body):
        weeks = [w for w in range(n_week) if LOCAL[u][w] is not None]
        if len({LOCAL[u][w] for w in weeks}) == 1 and len(weeks) == n_week:
            body(weeks[0])
        else:
            for w in weeks:
                pl.when(week == w)(functools.partial(body, w))

    slabs = (mine, far)
    side_of = jnp.where(row == 2, 1, 0)
    members = 2 * n_col
    chunk = 2 * length // members
    slices = pivot_ref.shape[0]

    def op_rows(op):
        return pl.ds(op * length, length)

    def low_copy(src, j, op, i, device):
        return remote(src, low_s.at[j, op, i], low_r.at[j, op], device, low.at[j, op_rows(op), :])

    def high_copy(src, j, op, i, device):
        return remote(src, high_s.at[j, op, i], high_r.at[j, op], device, high.at[j, op_rows(op), :])

    def to_week(w):
        return {WEEK: jnp.int32(w)}

    def pivot_out():
        return remote(pivot_ref, piv_s.at[0], piv_r.at[0], {ROW: pair}, piv.at[1])

    def local_copy(src, dst, i):
        return pltpu.make_async_copy(src, dst, loc.at[i])

    def weight_copy(k):
        return remote(weight_ref, wt_s.at[k - 1], wt_r.at[k - 1], {WEEK: lax.rem(week + k, n_week)}, wall.at[week])

    ROLES = ((1, 0, 1, 0, 2, 1), (2, 1, 2, 3, 1, 0))

    def by_role(body):
        for w, *role in ROLES:
            pl.when(week == w)(functools.partial(body, *role))

    def early():
        for k in range(1, n_week):
            weight_copy(k).start()
        pltpu.make_async_copy(weight_ref, wall.at[week], wt_s.at[n_week - 1]).start()

        @pl.when(outside)
        def _():
            by_role(lambda op, lag, *_: low_copy(x_ref.at[lag], 1, op, 0, {ROW: pair}).start())
            pivot_out().start()

        @pl.when(inside)
        def _():
            local_copy(pivot_ref, piv.at[0], 0).start()

            def send(op, lag, near, across, _):
                low_copy(x_ref.at[lag], 0, op, 0, to_week(across)).start()
                low_copy(x_ref.at[lag], 0, op, 1, to_week(near)).start()
                local_copy(x_ref.at[lag], low.at[0, op_rows(op), :], 1).start()

            by_role(send)

    def spread_low():
        def send(op, lag, near, across, theirs):
            ref = low.at[1, op_rows(op), :]
            low_copy(ref, 1, op, 0, to_week(across)).wait_recv()
            low_copy(ref, 1, op, 0, to_week(across)).start()
            low_copy(ref, 1, op, 1, to_week(near)).start()
            for j in range(2):
                ref = low.at[j, op_rows(theirs), :]
                low_copy(ref, j, theirs, 0, to_week(near)).wait_recv()
                low_copy(ref, j, theirs, 0, to_week(near)).start()
            local_copy(x_ref.at[lag], low.at[0, op_rows(op), :], 1).wait()

        by_role(send)

        @pl.when(edge)
        def _():
            for j in range(2):
                for op in range(2):
                    low_copy(low.at[j, op_rows(op), :], j, op, 0, to_week(1)).wait_recv()

        pivot_out().wait_recv()
        local_copy(pivot_ref, piv.at[0], 0).wait()

    def rows_of(m, count=1):
        return pl.ds(pl.multiple_of(m * chunk, chunk), count * chunk)

    def half_copy():
        away = rows_of((1 - side_of) * n_col, n_col)
        return remote(part.at[away, :], half_s.at[0], half_r.at[0], {ROW: opp}, came_z)

    def sum_copy(k):
        to = lax.rem(col + k, n_col)
        return remote(part.at[rows_of(side_of * n_col + to), :], sum_s.at[k - 1], sum_r.at[k - 1], {COL: to},
                      came_y.at[k - 1])

    me = side_of * n_col + col

    def all_copy(k):
        return remote(whole.at[rows_of(me), :], all_s.at[k - 1], all_r.at[k - 1], {COL: lax.rem(col + k, n_col)})

    def back_copy(k):
        ref = whole.at[rows_of(side_of * n_col + other(k)), :]
        return remote(ref, back_s.at[k], back_r.at[k], {ROW: opp})

    def make_part():
        def fill(m):
            at = rows_of(m)
            total = contract_last(low[0, at, :], piv[0]) + contract_last(low[1, at, :], piv[1])
            part[at, :] = total.astype(part.dtype)

        @pl.loop(0, n_col)
        def _(m):
            fill((1 - side_of) * n_col + m)

        half_copy().start()

        @pl.loop(0, n_col)
        def _(m):
            fill(side_of * n_col + m)

    def add_half():
        half_copy().wait_recv()

        @pl.loop(0, n_col)
        def _(m):
            at, here = rows_of(side_of * n_col + m), rows_of(m)
            total = part[at, :].astype(jnp.float32) + came_z[here, :].astype(jnp.float32)
            part[at, :] = total.astype(part.dtype)

        for k in peers:
            sum_copy(k).start()

    def make_whole():
        for k in peers:
            sum_copy(k).wait_recv()
        total = part[rows_of(me), :].astype(jnp.float32)
        for k in peers:
            total = total + came_y[k - 1].astype(jnp.float32)
        whole[rows_of(me), :] = total.astype(whole.dtype)
        back_copy(0).start()
        for k in peers:
            all_copy(k).start()

    def pass_whole():
        for k in peers:
            all_copy(k).wait_recv()
            back_copy(k).start()

    def column(slot, s):
        return f_ref.at[slot, :, pl.ds(pl.multiple_of(s * width, width), width)]

    def start_high():
        @pl.when(middle)
        def _():
            for s in slabs:
                ref = cell(0, 0, s)
                remote(ref, flow_s.at[0, s], flow_r.at[3, s], {ROW: pair}).wait_recv()

        @pl.when(week == 1)
        def _():
            for j, s in enumerate(slabs):
                high_copy(column(0, s), j, 0, 0, to_week(2)).start()
                high_copy(column(0, s), j, 0, 1, to_week(0)).start()
                high_copy(column(1, s), j, 1, 0, to_week(0)).start()
                local_copy(column(0, s), high.at[j, op_rows(0), :], 2 + j).start()
                local_copy(column(1, s), high.at[j, op_rows(1), :], 4 + j).start()

        @pl.when(week == 2)
        def _():
            for j, s in enumerate(slabs):
                high_copy(column(3, s), j, 1, 0, to_week(3)).start()
                local_copy(column(3, s), high.at[j, op_rows(1), :], 4 + j).start()

    def wait_high():
        for j, s in enumerate(slabs):
            @pl.when(week == 1)
            def _(j=j, s=s):
                local_copy(column(0, s), high.at[j, op_rows(0), :], 2 + j).wait()

            @pl.when(week != 1)
            def _(j=j):
                high_copy(high.at[j, op_rows(0), :], j, 0, 0, to_week(3)).wait_recv()

            @pl.when(week == 2)
            def _(j=j):
                high_copy(high.at[j, op_rows(0), :], j, 0, 0, to_week(3)).start()

            @pl.when(middle)
            def _(j=j, s=s):
                local_copy(column(1, s), high.at[j, op_rows(1), :], 4 + j).wait()

            @pl.when(edge)
            def _(j=j):
                high_copy(high.at[j, op_rows(1), :], j, 1, 0, to_week(3)).wait_recv()

    def panel_out():
        return remote(pan.at[1], pan_s.at[0], pan_r.at[0], {ROW: pair}, panel_ref)

    def inner_near(j):
        return remote(inn.at[j], inn_s.at[j], inn_r.at[j], {WEEK: jnp.where(week == 0, 1, 2)}, inn_in.at[j])

    def inner_far(j, i):
        device = {WEEK: jnp.int32(1)} if j == 0 else {WEEK: jnp.int32(1), ROW: pair}
        return remote(inn.at[j], inn_s.at[j], inn_r.at[2 + i], device, inner_ref.at[i])

    def own_weight():
        return pltpu.make_async_copy(weight_ref, wall.at[week], wt_s.at[n_week - 1])

    def turn_high():
        wait_high()
        for k in range(1, n_week):
            weight_copy(k).wait_recv()
        own_weight().wait()
        step = min(length, 512)
        for j in range(2):
            for op in range(2):
                for at in range(0, length, step):
                    rows = pl.ds(op * length + at, step)
                    flat = high[j, rows, :].T.astype(jnp.float32) * wall[1 + op, 1 + op, pl.ds(at, step)][None, :]
                    turned[j, :, rows] = flat.astype(turned.dtype)

    tile = min(slices, 256)

    def wait_whole():
        for k in range(n_col):
            back_copy(k).wait_recv()

    def make_panel(j):
        @pl.loop(0, slices // tile)
        def _(i):
            at = pl.ds(pl.multiple_of(i * tile, tile), tile)
            pan[j, :, at] = jnp.dot(turned[j], whole[:, at], preferred_element_type=jnp.float32).astype(pan.dtype)

        if j == 0:
            local_copy(pan.at[0], panel_ref, 0).start()
        else:
            panel_out().start()

    def make_inner(j):
        @pl.loop(0, 2 * length // tile)
        def _(i):
            at = pl.ds(pl.multiple_of(i * tile, tile), tile)
            inn[j, :, at] = contract_last(pan[j], whole[at, :]).astype(inn.dtype)

        pl.when(edge)(lambda: inner_near(j).start())

    def join_inner(j):
        @pl.when(middle)
        def _():
            inner_near(j).wait_recv()
            inn[j] = (inn[j].astype(jnp.float32) + inn_in[j].astype(jnp.float32)).astype(inn.dtype)
            pl.when(week == 2)(lambda: inner_far(j, 1).start())

            @pl.when(week == 1)
            def _():
                if j == 1:
                    inner_far(1, 0).start()
                else:
                    local_copy(inn.at[0], inner_ref.at[0], 1).start()

    first("start")
    for u in range(UNITS):
        local(u, lambda w, u=u: take(u, w).start())
    early()
    for u in range(UNITS):
        def move(w, u=u):
            take(u, w).wait()
            put(u).start()

        local(u, move)

    for u in range(UNITS):
        local(u, lambda w, u=u: put(u).wait())
        for _, _, _, week_of, unit in FIRST:
            if unit == u:
                @pl.when(week == week_of)
                def _(u=u):
                    remote(place(u, mine), first_s.at[u], first_r.at[u], {ROW: pair}).wait_recv()

        def begin(u=u):
            @pl.when(inside)
            def _():
                to_opp(u, mine, 0).start()
                to_pair(u, mine, 0).start()

            pl.when(outside)(lambda: to_pair(u, mine, 1).start())
            aside(u, mine, 0)

        active(u, begin)
        spread(u, mine)

    def from_side(u, at_row, hop, onward=None):
        def body():
            for k in peers:
                side(u, mine, hop, k).wait_recv()
                if onward is not None:
                    onward(k)
                spread(u, slab(at_row, other(k)))

        active(u, body)

    def arrived(u, s, hop, then):
        def body():
            to_pair(u, s, hop).wait_recv()
            then()
            spread(u, s)

        active(u, body)

    @pl.when(outside)
    def _():
        for u in range(UNITS):
            from_side(u, row, 0, lambda k, u=u: cross(u, k).start())
        for hop, at_row in enumerate((pair, opp, end)):
            s = slab(at_row, col)
            for u in range(UNITS):
                arrived(u, s, hop, lambda u=u, s=s, hop=hop: aside(u, s, hop + 1))
                if hop:
                    from_side(u, (pair, opp)[hop - 1], hop)
            if hop:
                relays((row, pair)[hop - 1])
        for u in range(UNITS):
            from_side(u, end, 3)
        relays(opp)
        relays(end)

    @pl.when(inside)
    def _():
        def cross_in(u):
            def body():
                for k in peers:
                    cross(u, k).wait_recv()
                    spread(u, slab(pair, other(k)))

            active(u, body)

        def near_one(u):
            s = slab(opp, col)

            def then():
                to_pair(u, s, 1).start()
                aside(u, s, 1)

            arrived(u, s, 0, then)

        def far_one(u):
            s = slab(end, col)

            def then():
                to_pair(u, s, 2).start()
                aside(u, s, 2)

            arrived(u, s, 2, then)

        for u in range(UNITS):
            near_one(u)
        spread_low()
        make_part()
        for u in range(UNITS):
            arrived(u, far, 1, lambda u=u: to_opp(u, far, 2).start())
            from_side(u, row, 0)
            if u == 2:
                add_half()
        make_whole()
        start_high()
        for u in range(UNITS):
            far_one(u)
            if u == 0:
                pass_whole()
            if u == 1:
                turn_high()
            if u == 2:
                wait_whole()
                make_panel(1)
                make_panel(0)
        make_inner(1)
        make_inner(0)
        for u in range(UNITS):
            cross_in(u)
            from_side(u, opp, 1)
        for j in (1, 0):
            join_inner(j)
        relays(row)
        relays(pair)
        for u in range(UNITS):
            from_side(u, end, 2)
        relays(opp)
        relays(end)

    @pl.when(middle)
    def _():
        for s in range(n):
            for flow in range(FLOWS):
                def arrive(s=s, flow=flow):
                    ref = cell(0, 0, s)
                    remote(ref, flow_s.at[0, s], flow_r.at[flow, s], {ROW: pair}).wait_recv()

                if flow == 3:
                    pl.when(outside | ((mine != s) & (far != s)))(arrive)
                else:
                    arrive()

    @pl.when(week == 1)
    def _():
        inner_far(1, 1).wait_recv()
        pl.when(outside)(lambda: inner_far(1, 0).wait_recv())

    @pl.when(outside)
    def _():
        panel_out().wait_recv()
        for k in range(1, n_week):
            weight_copy(k).wait_recv()
        own_weight().wait()
        by_role(lambda op, lag, *_: low_copy(x_ref.at[lag], 1, op, 0, {ROW: pair}).wait_send())
        pivot_out().wait_send()

    weights_out = pltpu.make_async_copy(wall, weights_ref, wt_s.at[n_week - 1])
    weights_out.start()
    for k in range(1, n_week):
        weight_copy(k).wait_send()

    @pl.when(inside)
    def _():
        def sent(op, lag, near, across, theirs):
            for j in range(2):
                for i in range(2):
                    low_copy(x_ref.at[0], j, op, i, to_week(0)).wait_send()
                low_copy(x_ref.at[0], j, theirs, 0, to_week(0)).wait_send()

        by_role(sent)
        half_copy().wait_send()
        for k in peers:
            sum_copy(k).wait_send()
            all_copy(k).wait_send()
        for k in range(n_col):
            back_copy(k).wait_send()

        @pl.when(week == 1)
        def _():
            for j, s in enumerate(slabs):
                high_copy(column(0, s), j, 0, 0, to_week(2)).wait_send()
                high_copy(column(0, s), j, 0, 1, to_week(0)).wait_send()
                high_copy(column(1, s), j, 1, 0, to_week(0)).wait_send()

        @pl.when(week == 2)
        def _():
            for j, s in enumerate(slabs):
                high_copy(column(3, s), j, 1, 0, to_week(3)).wait_send()
                high_copy(high.at[j, op_rows(0), :], j, 0, 0, to_week(3)).wait_send()

        local_copy(pan.at[0], panel_ref, 0).wait()
        panel_out().wait_send()
        for j in range(2):
            pl.when(edge)(lambda j=j: inner_near(j).wait_send())
            pl.when(week == 2)(lambda j=j: inner_far(j, 1).wait_send())

        @pl.when(week == 1)
        def _():
            inner_far(1, 0).wait_send()
            local_copy(inn.at[0], inner_ref.at[0], 1).wait()

    first("wait")
    for u in range(UNITS):
        def finish(u=u):
            for k in peers:
                for hop in range(3):
                    side(u, mine, hop, k).wait_send()

            @pl.when(outside)
            def _():
                to_pair(u, mine, 1).wait_send()
                for k in peers:
                    side(u, mine, 3, k).wait_send()
                    cross(u, k).wait_send()

            @pl.when(inside)
            def _():
                to_opp(u, mine, 0).wait_send()
                to_opp(u, far, 2).wait_send()
                for hop in range(3):
                    to_pair(u, mine, hop).wait_send()

        active(u, finish)
        if u >= 2:
            for s in range(n):
                spread(u, s, "wait")
    for s in range(n):
        relay(s, "wait")
    weights_out.wait()


def gather(x, pivot, weight, collective_id):
    n_row, n_col = lax.axis_size(ROW), lax.axis_size(COL)
    _, length, width = x.shape
    slices = pivot.shape[0]
    n = n_row * n_col
    assert n_row == 4 and lax.axis_size(WEEK) == 4
    sides = (UNITS, n_col - 1)
    vmem = functools.partial(lambda *shape: pltpu.VMEM(shape, x.dtype))
    sent = length * width * 2 * (n - 1) * 9 // 4
    hbm = pl.BlockSpec(memory_space=pl.ANY)
    return pl.pallas_call(
        functools.partial(gather_kernel, n_row, n_col),
        out_shape=(
            jax.ShapeDtypeStruct((5, length, width * n), x.dtype),
            jax.ShapeDtypeStruct((width, slices), x.dtype),
            jax.ShapeDtypeStruct((2, width, 2 * length), x.dtype),
            jax.ShapeDtypeStruct((4, *weight.shape), weight.dtype),
        ),
        in_specs=[hbm] * 3,
        out_specs=(hbm,) * 4,
        scratch_shapes=[
            pltpu.VMEM((UNITS, length // 2, width), x.dtype), DMA((UNITS,)), DMA((UNITS,)), DMA((UNITS,)),
            DMA((UNITS, 3)), DMA((UNITS, 3)), DMA((UNITS, 3)), DMA(sides), DMA(sides),
            DMA((UNITS, 4, n_col - 1)), DMA((UNITS, 4, n_col - 1)), DMA((5, n)), DMA((FLOWS, n)),
            vmem(2, 2 * length, width), vmem(2, slices, width), vmem(2, 2 * length, width),
            vmem(2 * length, slices), vmem(length, slices), vmem(n_col - 1, length // n_col, slices),
            vmem(2 * length, slices),
            vmem(2, width, 2 * length), vmem(2, width, slices), vmem(2, width, 2 * length),
            vmem(2, width, 2 * length), pltpu.VMEM((4, *weight.shape), weight.dtype),
            DMA((2, 2, 2)), DMA((2, 2)), DMA((1,)), DMA((1,)), DMA((2, 2, 2)), DMA((2, 2)), DMA((6,)),
            DMA((1,)), DMA((1,)), DMA((n_col - 1,)), DMA((n_col - 1,)),
            DMA((n_col - 1,)), DMA((n_col - 1,)), DMA((n_col,)), DMA((n_col,)),
            DMA((1,)), DMA((1,)), DMA((2,)), DMA((4,)), DMA((4,)), DMA((3,)),
        ],
        compiler_params=pltpu.CompilerParams(
            collective_id=collective_id, has_side_effects=True, vmem_limit_bytes=60 << 20),
        cost_estimate=pl.CostEstimate(flops=0, bytes_accessed=sent * 8, transcendentals=0),
    )(x, pivot, weight)


PRODUCTS = ((0, 0, 0, (0, 3)), (0, 1, 1, (0, 2)), (0, 2, 2, (0, 1)), (1, 0, 3, (1, 3)), (1, 1, 4, (1, 2)),
            (2, 0, 2, (2, 3)))


def bands_kernel(at_ref, left_ref, weight_ref, prior_ref, full_ref, out_ref, turned):
    week, mine = at_ref[0], at_ref[1]
    tile = pl.program_id(0)
    width = left_ref.shape[2]
    columns = full_ref.shape[2]

    @pl.when(tile == 0)
    def _():
        for p, (_, slot, _, (lo, hi)) in enumerate(PRODUCTS):
            @pl.when((week >= lo) & (week <= hi))
            def _(p=p, slot=slot):
                flat = left_ref[slot].T.astype(jnp.float32) * weight_ref[p][None, :]
                turned[p] = flat.astype(turned.dtype)

    out_ref[...] = jnp.zeros_like(out_ref)
    for p, (band, _, slot, (lo, hi)) in enumerate(PRODUCTS):
        @pl.when((week >= lo) & (week <= hi))
        def _(p=p, band=band, slot=slot):
            out_ref[band] += jnp.dot(turned[p], full_ref[slot], preferred_element_type=jnp.float32)

    row_ids = lax.broadcasted_iota(jnp.int32, (width, columns), 0) + mine * width
    col_ids = lax.broadcasted_iota(jnp.int32, (width, columns), 1) + tile * columns
    out_ref[0] += jnp.where(row_ids == col_ids, prior_ref[:, :1], 0.0)


def bands(at, full, weights, prior):
    slots, length, regions = full.shape
    width = prior.shape[0]
    columns = min(512, regions)
    return pl.pallas_call(
        bands_kernel,
        out_shape=jax.ShapeDtypeStruct((3, width, regions), jnp.float32),
        grid_spec=pltpu.PrefetchScalarGridSpec(
            num_scalar_prefetch=1,
            grid=(regions // columns,),
            in_specs=[
                pl.BlockSpec((3, length, width), lambda j, at: (0, 0, at[1]), pipeline_mode=pl.Buffered(1)),
                pl.BlockSpec(weights.shape, lambda j, at: (0, 0)),
                pl.BlockSpec(prior.shape, lambda j, at: (0, 0)),
                pl.BlockSpec((slots, length, columns), lambda j, at: (0, 0, j)),
            ],
            out_specs=pl.BlockSpec((3, width, columns), lambda j, at: (0, 0, j)),
            scratch_shapes=[pltpu.VMEM((len(PRODUCTS), width, length), full.dtype)],
        ),
        compiler_params=pltpu.CompilerParams(dimension_semantics=("arbitrary",), vmem_limit_bytes=60 << 20),
        cost_estimate=pl.CostEstimate(
            flops=10 * width * length * regions, bytes_accessed=full.size * 2 + 12 * width * regions,
            transcendentals=0),
    )(at, full, weights, prior, full)


def schur_kernel(at_ref, left_ref, weight_ref, prior_ref, inner_ref, full_ref, out_ref, turned):
    week, mine = at_ref[0], at_ref[1]
    tile = pl.program_id(0)
    slots, length, width = left_ref.shape
    columns = full_ref.shape[2]

    @pl.when(week == 1)
    def _():
        @pl.when(tile == 0)
        def _():
            for k in range(slots):
                flat = left_ref[k].T.astype(jnp.float32) * weight_ref[k][None, :]
                if k < 2:
                    at = pl.ds(k * length, length)
                    inner = inner_ref[0, :, at].astype(jnp.float32) + inner_ref[1, :, at].astype(jnp.float32)
                    flat = flat - inner * weight_ref[3 + k][None, :]
                turned[k] = flat.astype(turned.dtype)

        total = jnp.dot(turned[0], full_ref[0], preferred_element_type=jnp.float32)
        for k in range(1, slots):
            total = total + jnp.dot(turned[k], full_ref[k], preferred_element_type=jnp.float32)
        row_ids = lax.broadcasted_iota(jnp.int32, (width, columns), 0) + mine * width
        col_ids = lax.broadcasted_iota(jnp.int32, (width, columns), 1) + tile * columns
        total = total + jnp.where(row_ids == col_ids, prior_ref[:, :1], 0.0)
        out_ref[...] = total.astype(out_ref.dtype)


def schur_rows(at, full, weights, prior, inner):
    _, length, regions = full.shape
    width = prior.shape[0]
    columns = min(512, regions)
    whole = pl.Buffered(1)
    return pl.pallas_call(
        schur_kernel,
        out_shape=jax.ShapeDtypeStruct((width, regions), jnp.bfloat16),
        grid_spec=pltpu.PrefetchScalarGridSpec(
            num_scalar_prefetch=1,
            grid=(regions // columns,),
            in_specs=[
                pl.BlockSpec((3, length, width), lambda j, at: (0, 0, at[1]), pipeline_mode=whole),
                pl.BlockSpec(weights.shape, lambda j, at: (0, 0)),
                pl.BlockSpec(prior.shape, lambda j, at: (0, 0)),
                pl.BlockSpec(inner.shape, lambda j, at: (0, 0, 0), pipeline_mode=whole),
                pl.BlockSpec((3, length, columns), lambda j, at: (0, 0, jnp.where(at[0] == 1, j, 0))),
            ],
            out_specs=pl.BlockSpec((width, columns), lambda j, at: (0, j)),
            scratch_shapes=[pltpu.VMEM((3, width, length), full.dtype)],
        ),
        compiler_params=pltpu.CompilerParams(dimension_semantics=("arbitrary",), vmem_limit_bytes=60 << 20),
        cost_estimate=pl.CostEstimate(
            flops=6 * width * length * regions, bytes_accessed=6 * length * regions, transcendentals=0),
    )(at, full, weights, prior, inner, full)


def body(sensitivity, reach, obs_weight, prior_precision, pivot_solve):
    week = lax.axis_index(WEEK)
    n_week, n_col = lax.axis_size(WEEK), lax.axis_size(COL)
    local = sensitivity[0]
    lags, length, width = local.shape
    mine = lax.axis_index(ROW) * n_col + lax.axis_index(COL)

    lag = jnp.arange(8)[:, None]
    own_weight = jnp.where((reach >= lag) & (week >= lag) & (lag < lags), obs_weight, 0.0)
    full, panel, inner, by_week = gather(local, pivot_solve, own_weight, 0)
    by_week = by_week[:, :lags]
    later = jnp.concatenate([by_week, jnp.zeros((lags, lags, length), by_week.dtype)])
    here = lax.dynamic_slice(later, (week, 0, 0), (lags, lags, length))
    weights = jnp.stack([here[0, 0], here[1, 1], here[2, 2], here[0, 1], here[1, 2], here[0, 2]])

    at = jnp.stack([week, mine]).astype(jnp.int32)
    prior = jnp.broadcast_to(prior_precision[0][:, None], (width, 128))
    out = schur_rows(at, full, weights, prior, inner)
    quarter = out.shape[1] // n_week
    schur = out[:, quarter : 2 * quarter]
    moved = [(w, lax.ppermute(out[:, w * quarter : (w + 1) * quarter], WEEK, [(1, w)])) for w in (2, 3, 0)]
    h = bands(at, full, weights, prior)
    for w, block in moved:
        schur = jnp.where(week == w, block, schur)
    return (h[None], panel, schur.astype(jnp.float32))


def solution(mesh):
    placed = (
        P(WEEK, None, None, (ROW, COL)),
        P(WEEK, None),
        P(WEEK, None),
        P(WEEK, (ROW, COL)),
        P(WEEK, (ROW, COL)),
    )
    return jax.shard_map(
        body,
        mesh=mesh,
        in_specs=placed,
        out_specs=(
            P(WEEK, None, (ROW, COL), None),
            P((ROW, COL), WEEK),
            P((ROW, COL), WEEK),
        ),
        check_vma=False,
    )
```

time: 398 us -> 394 us (0.990)
  the two profiles are of different devices: /device:TPU:17 before, /device:TPU:5 now
where the time goes in v2:
time: 394 us; the launch traced here: 393 us
  Pallas kernels  376 us (95%)
  local copies, waits for them, and re-layouts  6.9 us (2%)
  starting transfers between devices  4.97 us (1%)
  other arithmetic  4.88 us (1%)
    pallas_call x1, Pallas kernels, gather(): pl.pallas_call(functools.partial(gather_kernel, n_row, n_col), out_shape=...  314 us
    pallas_call x1, Pallas kernels, bands(): pl.pallas_call(bands_kernel, out_shape=jax.ShapeDtypeStruct((3, width, re...  39 us
    pallas_call x1, Pallas kernels, schur_rows(): pl.pallas_call(schur_kernel, out_shape=jax.ShapeDtypeStruct((width, regio...  22.8 us
  transfers between devices with their start and end apart: 3, of which 0 were waited for; matrix products, arithmetic and copies ran while one was open for 0% of the time, Pallas kernels for 10%

profile of v2, /device:TPU:5, one launch (start us, length us, event | category | flops | bytes accessed | tf_op | source)
XLA Modules:
  0.0 393.2 jit_solution(17537876445375852469)
XLA Ops:
  0.6 0.0 copy-start.1
  0.7 1.4 fusion.5.weight_ref
  2.1 314.0 %shard_map.76 = (bf16[5,1024,4096]{2,1,0:T(8,128)(2,1)}, bf16[512,1024]{1,0:T(8,128)(2,1)}, bf16[2,512,2048]{2,1,0:T(8,128)(2,1)}, f32[4,8,1024]{2,1,0:T(8,128)}) custom-call(bf16[3,1024,512]{2,1,0:T(8,128)(2,1)} %bitcast.20, bf16[1024,512]{1,0:T(8,128)(2,1)} %pivot_ref.1, f32[8,1024]{1,0:T(8,128)} %fusion.5.weight_ref), custom_call_target="tpu_custom_call" | custom-call | bytes 132120576 | tf_op jit(solution)/shard_map/pallas_call | solution.py:668
  316.0 0.9 slice.33
  317.0 0.6 pad_add_fusion.at_ref
  317.6 0.7 stack.15.weight_ref
  318.3 0.0 copy-done.1
  318.3 0.8 broadcast_in_dim.30.prior_ref
  319.1 22.8 %shard_map.78 = bf16[512,4096]{1,0:T(8,128)(2,1)} custom-call(s32[2]{0:T(128)} %pad_add_fusion.at_ref, bf16[5,1024,4096]{2,1,0:T(8,128)(2,1)} %get-tuple-element.7.left_ref.full_ref, f32[6,1024]{1,0:T(8,128)} %stack.15.weight_ref, f32[512,128]{1,0:T(8,128)} %broadcast_in_dim.30.prior_ref, bf16[2,512,2048]{2,1,0:T(8,128)(2,1)} %get-tuple-element.10.inner_ref, ...), custom_call_target="tpu_custom_call" | custom-call | flops 12884901888 | bytes 25165824 | tf_op jit(solution)/shard_map/pallas_call | solution.py:785
  341.9 3.5 fusion.12
  345.4 1.3 collective-permute-start
  346.7 1.4 collective-permute-start.1
  348.1 2.3 collective-permute-start.2
  350.3 39.0 %shard_map.77 = f32[3,512,4096]{2,1,0:T(8,128)} custom-call(s32[2]{0:T(128)} %pad_add_fusion.at_ref, bf16[5,1024,4096]{2,1,0:T(8,128)(2,1)} %get-tuple-element.7.left_ref.full_ref, f32[6,1024]{1,0:T(8,128)} %stack.15.weight_ref, f32[512,128]{1,0:T(8,128)} %broadcast_in_dim.30.prior_ref, bf16[5,1024,4096]{2,1,0:T(8,128)(2,1)} %get-tuple-element.7.left_ref.full_ref), custom_call_target="tpu_custom_call" | custom-call | flops 21474836480 | bytes 67108864 | tf_op jit(solution)/shard_map/pallas_call | solution.py:731
  389.3 0.0 copy-start
  389.3 0.0 collective-permute-done
  389.3 0.0 collective-permute-done.1
  389.3 0.0 collective-permute-done.2
  389.3 2.9 fusion.2
  392.2 0.0 copy-done
  392.2 1.0 copy.9
  (2 shorter events, 0.0 us)
Async XLA Ops:
  0.6 317.6 %copy-start.1 = (f32[1,512]{1,0:T(1,128)S(1)}, f32[1,512]{1,0:T(1,128)}, u32[]{:S(2)}) copy-start(f32[1,512]{1,0:T(1,128)} %param.8) | copy-start | bytes 6148
  345.4 44.0 %collective-permute-start = (bf16[512,1024]{1,0:T(8,128)(2,1)}, bf16[512,1024]{1,0:T(8,128)(2,1)S(1)}, u32[]{:S(2)}, u32[]{:S(2)}) collective-permute-start(bf16[512,1024]{1,0:T(8,128)(2,1)} %get-tuple-element.13), channel_id=1, source_target_pairs={{8,0},{9,1},{10,2},{11,3},{12,4},{13,5},{14,6},{15,7}} | collective-permute-start | bytes 3145736 | tf_op jit(solution)/shard_map/ppermute | solution.py:827
  346.7 42.6 %collective-permute-start.1 = (bf16[512,1024]{1,0:T(8,128)(2,1)}, bf16[512,1024]{1,0:T(8,128)(2,1)S(1)}, u32[]{:S(2)}, u32[]{:S(2)}) collective-permute-start(bf16[512,1024]{1,0:T(8,128)(2,1)} %get-tuple-element.12), channel_id=1, source_target_pairs={{8,24},{9,25},{10,26},{11,27},{12,28},{13,29},{14,30},{15,31}} | collective-permute-start | bytes 3145736 | tf_op jit(solution)/shard_map/ppermute | solution.py:827
  348.1 41.2 %collective-permute-start.2 = (bf16[512,1024]{1,0:T(8,128)(2,1)S(1)}, bf16[512,1024]{1,0:T(8,128)(2,1)}, u32[]{:S(2)}, u32[]{:S(2)}) collective-permute-start(bf16[512,1024]{1,0:T(8,128)(2,1)S(1)} %get-tuple-element.11), channel_id=1, source_target_pairs={{8,16},{9,17},{10,18},{11,19},{12,20},{13,21},{14,22},{15,23}} | collective-permute-start | bytes 3145736 | tf_op jit(solution)/shard_map/ppermute | solution.py:827
  389.3 2.9 copy-start

commit v3 on v2

--- a/solution.py
+++ b/solution.py
@@ -250,9 +250,9 @@
     def rows_of(m, count=1):
         return pl.ds(pl.multiple_of(m * chunk, chunk), count * chunk)
 
-    def half_copy():
-        away = rows_of((1 - side_of) * n_col, n_col)
-        return remote(part.at[away, :], half_s.at[0], half_r.at[0], {ROW: opp}, came_z)
+    def half_copy(k):
+        away = rows_of((1 - side_of) * n_col + lax.rem(col + k, n_col))
+        return remote(part.at[away, :], half_s.at[k], half_r.at[k], {ROW: opp}, came_z.at[k])
 
     def sum_copy(k):
         to = lax.rem(col + k, n_col)
@@ -267,6 +267,8 @@
     def back_copy(k):
         ref = whole.at[rows_of(side_of * n_col + other(k)), :]
         return remote(ref, back_s.at[k], back_r.at[k], {ROW: opp})
+
+    by_turn = (*peers, 0)
 
     def make_part():
         def fill(m):
@@ -274,26 +276,20 @@
             total = contract_last(low[0, at, :], piv[0]) + contract_last(low[1, at, :], piv[1])
             part[at, :] = total.astype(part.dtype)
 
-        @pl.loop(0, n_col)
-        def _(m):
-            fill((1 - side_of) * n_col + m)
-
-        half_copy().start()
+        for k in by_turn:
+            fill((1 - side_of) * n_col + lax.rem(col + k, n_col))
+            half_copy(k).start()
 
         @pl.loop(0, n_col)
         def _(m):
             fill(side_of * n_col + m)
 
-    def add_half():
-        half_copy().wait_recv()
-
-        @pl.loop(0, n_col)
-        def _(m):
-            at, here = rows_of(side_of * n_col + m), rows_of(m)
-            total = part[at, :].astype(jnp.float32) + came_z[here, :].astype(jnp.float32)
-            part[at, :] = total.astype(part.dtype)
-
-        for k in peers:
+    def add_half(k):
+        half_copy(k).wait_recv()
+        at = rows_of(side_of * n_col + lax.rem(col + k, n_col))
+        total = part[at, :].astype(jnp.float32) + came_z[k].astype(jnp.float32)
+        part[at, :] = total.astype(part.dtype)
+        if k:
             sum_copy(k).start()
 
     def make_whole():
@@ -453,7 +449,7 @@
             aside(u, mine, 0)
 
         active(u, begin)
-        spread(u, mine)
+        pl.when(outside)(lambda u=u: spread(u, mine))
 
     def from_side(u, at_row, hop, onward=None):
         def body():
@@ -483,8 +479,9 @@
                 arrived(u, s, hop, lambda u=u, s=s, hop=hop: aside(u, s, hop + 1))
                 if hop:
                     from_side(u, (pair, opp)[hop - 1], hop)
-            if hop:
-                relays((row, pair)[hop - 1])
+                if hop == 2 and u == 2:
+                    relays(row)
+                    relays(pair)
         for u in range(UNITS):
             from_side(u, end, 3)
         relays(opp)
@@ -518,36 +515,56 @@
 
             arrived(u, s, 2, then)
 
-        for u in range(UNITS):
-            near_one(u)
+        def pass_on(u):
+            active(u, lambda: to_opp(u, far, 2).start())
+
+        def outer_one(u):
+            arrived(u, far, 1, lambda: None)
+
+        near_one(0)
+        near_one(1)
         spread_low()
         make_part()
         for u in range(UNITS):
-            arrived(u, far, 1, lambda u=u: to_opp(u, far, 2).start())
+            spread(u, mine)
+        near_one(2)
+        for u in range(2):
+            outer_one(u)
+            pass_on(u)
+        for k in peers:
+            add_half(k)
+        for u in range(3, UNITS):
+            near_one(u)
+        for u in range(2, UNITS):
+            outer_one(u)
+        for u in range(UNITS):
             from_side(u, row, 0)
-            if u == 2:
-                add_half()
+        add_half(0)
         make_whole()
+        far_one(0)
+        pass_on(2)
+        far_one(1)
+        pass_whole()
+        for u in range(3, UNITS):
+            pass_on(u)
         start_high()
         for u in range(UNITS):
-            far_one(u)
-            if u == 0:
-                pass_whole()
-            if u == 1:
-                turn_high()
-            if u == 2:
-                wait_whole()
-                make_panel(1)
-                make_panel(0)
-        make_inner(1)
-        make_inner(0)
+            from_side(u, opp, 1)
         for u in range(UNITS):
             cross_in(u)
-            from_side(u, opp, 1)
-        for j in (1, 0):
-            join_inner(j)
+        far_one(2)
+        turn_high()
+        wait_whole()
+        make_panel(1)
+        make_inner(1)
+        make_panel(0)
+        make_inner(0)
+        for u in range(3, UNITS):
+            far_one(u)
         relays(row)
         relays(pair)
+        join_inner(1)
+        join_inner(0)
         for u in range(UNITS):
             from_side(u, end, 2)
         relays(opp)
@@ -594,7 +611,8 @@
                 low_copy(x_ref.at[0], j, theirs, 0, to_week(0)).wait_send()
 
         by_role(sent)
-        half_copy().wait_send()
+        for k in range(n_col):
+            half_copy(k).wait_send()
         for k in peers:
             sum_copy(k).wait_send()
             all_copy(k).wait_send()
@@ -680,12 +698,13 @@
             DMA((UNITS, 3)), DMA((UNITS, 3)), DMA((UNITS, 3)), DMA(sides), DMA(sides),
             DMA((UNITS, 4, n_col - 1)), DMA((UNITS, 4, n_col - 1)), DMA((5, n)), DMA((FLOWS, n)),
             vmem(2, 2 * length, width), vmem(2, slices, width), vmem(2, 2 * length, width),
-            vmem(2 * length, slices), vmem(length, slices), vmem(n_col - 1, length // n_col, slices),
+            vmem(2 * length, slices), vmem(n_col, length // n_col, slices),
+            vmem(n_col - 1, length // n_col, slices),
             vmem(2 * length, slices),
             vmem(2, width, 2 * length), vmem(2, width, slices), vmem(2, width, 2 * length),
             vmem(2, width, 2 * length), pltpu.VMEM((4, *weight.shape), weight.dtype),
             DMA((2, 2, 2)), DMA((2, 2)), DMA((1,)), DMA((1,)), DMA((2, 2, 2)), DMA((2, 2)), DMA((6,)),
-            DMA((1,)), DMA((1,)), DMA((n_col - 1,)), DMA((n_col - 1,)),
+            DMA((n_col,)), DMA((n_col,)), DMA((n_col - 1,)), DMA((n_col - 1,)),
             DMA((n_col - 1,)), DMA((n_col - 1,)), DMA((n_col,)), DMA((n_col,)),
             DMA((1,)), DMA((1,)), DMA((2,)), DMA((4,)), DMA((4,)), DMA((3,)),
         ],

time: 394 us -> 348 us (0.88)
  Pallas kernels: 376 us -> 330 us
    pallas_call x1, Pallas kernels: 314 us -> 269 us  [gather(): pl.pallas_call(functools.partial(gather_kernel, n_row, n_col), out_shape=...]
  transfers between devices with their start and end apart: 3 -> 3, of which waited for: 0 -> 0; matrix products, arithmetic and copies ran while one was open for 0% -> 0% of each run, Pallas kernels for 10% -> 11%
where the time goes in v3:
time: 348 us
  Pallas kernels  330 us (95%)
  local copies, waits for them, and re-layouts  6.9 us (2%)
  starting transfers between devices  4.97 us (1%)
  other arithmetic  4.88 us (1%)
    pallas_call x1, Pallas kernels, gather(): pl.pallas_call(functools.partial(gather_kernel, n_row, n_col), out_shape=...  269 us
    pallas_call x1, Pallas kernels, bands(): pl.pallas_call(bands_kernel, out_shape=jax.ShapeDtypeStruct((3, width, re...  39 us
    pallas_call x1, Pallas kernels, schur_rows(): pl.pallas_call(schur_kernel, out_shape=jax.ShapeDtypeStruct((width, regio...  22.8 us
  transfers between devices with their start and end apart: 3, of which 0 were waited for; matrix products, arithmetic and copies ran while one was open for 0% of the time, Pallas kernels for 11%

profile of v3, /device:TPU:5, one launch (start us, length us, event | category | flops | bytes accessed | tf_op | source)
XLA Modules:
  0.0 347.9 jit_solution(11842732114606810109)
XLA Ops:
  0.6 0.0 copy-start.1
  0.7 1.4 fusion.5.weight_ref
  2.1 268.7 %shard_map.76 = (bf16[5,1024,4096]{2,1,0:T(8,128)(2,1)}, bf16[512,1024]{1,0:T(8,128)(2,1)}, bf16[2,512,2048]{2,1,0:T(8,128)(2,1)}, f32[4,8,1024]{2,1,0:T(8,128)}) custom-call(bf16[3,1024,512]{2,1,0:T(8,128)(2,1)} %bitcast.20, bf16[1024,512]{1,0:T(8,128)(2,1)} %pivot_ref.1, f32[8,1024]{1,0:T(8,128)} %fusion.5.weight_ref), custom_call_target="tpu_custom_call" | custom-call | bytes 132120576 | tf_op jit(solution)/shard_map/pallas_call | solution.py:686
  270.7 0.9 slice.33
  271.7 0.6 pad_add_fusion.at_ref
  272.3 0.7 stack.15.weight_ref
  273.0 0.0 copy-done.1
  273.0 0.8 broadcast_in_dim.30.prior_ref
  273.8 22.8 %shard_map.78 = bf16[512,4096]{1,0:T(8,128)(2,1)} custom-call(s32[2]{0:T(128)} %pad_add_fusion.at_ref, bf16[5,1024,4096]{2,1,0:T(8,128)(2,1)} %get-tuple-element.7.left_ref.full_ref, f32[6,1024]{1,0:T(8,128)} %stack.15.weight_ref, f32[512,128]{1,0:T(8,128)} %broadcast_in_dim.30.prior_ref, bf16[2,512,2048]{2,1,0:T(8,128)(2,1)} %get-tuple-element.10.inner_ref, ...), custom_call_target="tpu_custom_call" | custom-call | flops 12884901888 | bytes 25165824 | tf_op jit(solution)/shard_map/pallas_call | solution.py:804
  296.6 3.5 %fusion.12 = (bf16[512,1024]{1,0:T(8,128)(2,1)S(1)}, bf16[512,1024]{1,0:T(8,128)(2,1)}, bf16[512,1024]{1,0:T(8,128)(2,1)}) fusion(bf16[512,4096]{1,0:T(8,128)(2,1)} %shard_map.78), kind=kLoop, calls=%fused_computation.23 | loop fusion | bytes 6291456 | tf_op jit(solution)/shard_map/slice | solution.py:846
  300.1 1.3 collective-permute-start
  301.4 1.4 collective-permute-start.1
  302.8 2.3 collective-permute-start.2
  305.1 39.0 %shard_map.77 = f32[3,512,4096]{2,1,0:T(8,128)} custom-call(s32[2]{0:T(128)} %pad_add_fusion.at_ref, bf16[5,1024,4096]{2,1,0:T(8,128)(2,1)} %get-tuple-element.7.left_ref.full_ref, f32[6,1024]{1,0:T(8,128)} %stack.15.weight_ref, f32[512,128]{1,0:T(8,128)} %broadcast_in_dim.30.prior_ref, bf16[5,1024,4096]{2,1,0:T(8,128)(2,1)} %get-tuple-element.7.left_ref.full_ref), custom_call_target="tpu_custom_call" | custom-call | flops 21474836480 | bytes 67108864 | tf_op jit(solution)/shard_map/pallas_call | solution.py:750
  344.0 0.0 copy-start
  344.0 0.0 collective-permute-done
  344.0 0.0 collective-permute-done.1
  344.0 0.0 collective-permute-done.2
  344.0 2.9 fusion.2
  346.9 0.0 copy-done
  346.9 1.0 copy.9
  (2 shorter events, 0.0 us)
Async XLA Ops:
  0.6 272.4 %copy-start.1 = (f32[1,512]{1,0:T(1,128)S(1)}, f32[1,512]{1,0:T(1,128)}, u32[]{:S(2)}) copy-start(f32[1,512]{1,0:T(1,128)} %param.8) | copy-start | bytes 6148
  300.1 43.9 %collective-permute-start = (bf16[512,1024]{1,0:T(8,128)(2,1)}, bf16[512,1024]{1,0:T(8,128)(2,1)S(1)}, u32[]{:S(2)}, u32[]{:S(2)}) collective-permute-start(bf16[512,1024]{1,0:T(8,128)(2,1)} %get-tuple-element.13), channel_id=1, source_target_pairs={{8,0},{9,1},{10,2},{11,3},{12,4},{13,5},{14,6},{15,7}} | collective-permute-start | bytes 3145736 | tf_op jit(solution)/shard_map/ppermute | solution.py:846
  301.4 42.6 %collective-permute-start.1 = (bf16[512,1024]{1,0:T(8,128)(2,1)}, bf16[512,1024]{1,0:T(8,128)(2,1)S(1)}, u32[]{:S(2)}, u32[]{:S(2)}) collective-permute-start(bf16[512,1024]{1,0:T(8,128)(2,1)} %get-tuple-element.12), channel_id=1, source_target_pairs={{8,24},{9,25},{10,26},{11,27},{12,28},{13,29},{14,30},{15,31}} | collective-permute-start | bytes 3145736 | tf_op jit(solution)/shard_map/ppermute | solution.py:846
  302.8 41.2 %collective-permute-start.2 = (bf16[512,1024]{1,0:T(8,128)(2,1)S(1)}, bf16[512,1024]{1,0:T(8,128)(2,1)}, u32[]{:S(2)}, u32[]{:S(2)}) collective-permute-start(bf16[512,1024]{1,0:T(8,128)(2,1)S(1)} %get-tuple-element.11), channel_id=1, source_target_pairs={{8,16},{9,17},{10,18},{11,19},{12,20},{13,21},{14,22},{15,23}} | collective-permute-start | bytes 3145736 | tf_op jit(solution)/shard_map/ppermute | solution.py:846
  344.0 2.9 copy-start

commit v4 on v3

--- a/solution.py
+++ b/solution.py
@@ -714,39 +714,73 @@
     )(x, pivot, weight)
 
 
-PRODUCTS = ((0, 0, 0, (0, 3)), (0, 1, 1, (0, 2)), (0, 2, 2, (0, 1)), (1, 0, 3, (1, 3)), (1, 1, 4, (1, 2)),
-            (2, 0, 2, (2, 3)))
-
-
-def bands_kernel(at_ref, left_ref, weight_ref, prior_ref, full_ref, out_ref, turned):
-    week, mine = at_ref[0], at_ref[1]
+TERMS = (
+    (((0, 0, 0), (1, 1, 1), (2, 2, 2)), (), ()),
+    (((0, 0, 0), (1, 1, 1), (2, 2, 2)), ((0, 3, 3), (1, 4, 4)), ()),
+    (((0, 0, 0), (1, 1, 1)), ((0, 3, 3), (1, 4, 4)), ((0, 2, 5),)),
+    (((0, 0, 0),), ((0, 3, 3),), ((0, 2, 5),)),
+)
+HAVE = tuple(tuple(any(right == slot for band in week for _, right, _ in band) for week in TERMS) for slot in range(5))
+
+
+def when_tile(at_ref, tile, columns, width, body):
+    first = at_ref[1] * width
+
+    @pl.when(first // columns == tile)
+    def _():
+        body(pl.ds(pl.multiple_of(lax.rem(first, columns), width), width))
+
+
+def diagonal(prior_ref, width):
+    rows = lax.broadcasted_iota(jnp.int32, (width, width), 0)
+    cols = lax.broadcasted_iota(jnp.int32, (width, width), 1)
+    return jnp.where(rows == cols, prior_ref[:, :1], 0.0)
+
+
+def bands_kernel(at_ref, left_ref, weight_ref, prior_ref, *refs):
+    full_refs, out_ref, turned = refs[:5], refs[5], refs[6]
+    week = at_ref[0]
     tile = pl.program_id(0)
     width = left_ref.shape[2]
-    columns = full_ref.shape[2]
-
-    @pl.when(tile == 0)
-    def _():
-        for p, (_, slot, _, (lo, hi)) in enumerate(PRODUCTS):
-            @pl.when((week >= lo) & (week <= hi))
-            def _(p=p, slot=slot):
-                flat = left_ref[slot].T.astype(jnp.float32) * weight_ref[p][None, :]
-                turned[p] = flat.astype(turned.dtype)
-
-    out_ref[...] = jnp.zeros_like(out_ref)
-    for p, (band, _, slot, (lo, hi)) in enumerate(PRODUCTS):
-        @pl.when((week >= lo) & (week <= hi))
-        def _(p=p, band=band, slot=slot):
-            out_ref[band] += jnp.dot(turned[p], full_ref[slot], preferred_element_type=jnp.float32)
-
-    row_ids = lax.broadcasted_iota(jnp.int32, (width, columns), 0) + mine * width
-    col_ids = lax.broadcasted_iota(jnp.int32, (width, columns), 1) + tile * columns
-    out_ref[0] += jnp.where(row_ids == col_ids, prior_ref[:, :1], 0.0)
-
-
-def bands(at, full, weights, prior):
+    columns = out_ref.shape[2]
+
+    for w, by_band in enumerate(TERMS):
+        @pl.when(week == w)
+        def _(by_band=by_band):
+            @pl.when(tile == 0)
+            def _():
+                for band in by_band:
+                    for slot, _, p in band:
+                        flat = left_ref[slot].T.astype(jnp.float32) * weight_ref[p][None, :]
+                        turned[p] = flat.astype(turned.dtype)
+
+            for i, band in enumerate(by_band):
+                if band:
+                    total = None
+                    for _, right, p in band:
+                        term = jnp.dot(turned[p], full_refs[right][...], preferred_element_type=jnp.float32)
+                        total = term if total is None else total + term
+                    out_ref[i] = total
+                else:
+                    out_ref[i] = jnp.zeros(out_ref.shape[1:], out_ref.dtype)
+
+    def add(at):
+        out_ref[0, :, at] += diagonal(prior_ref, width)
+
+    when_tile(at_ref, tile, columns, width, add)
+
+
+def bands(at, full, weights, prior, columns):
     slots, length, regions = full.shape
     width = prior.shape[0]
-    columns = min(512, regions)
+
+    def right(slot):
+        def index(j, at):
+            here = functools.reduce(jnp.logical_or, [at[0] == w for w in range(4) if HAVE[slot][w]])
+            return slot, 0, jnp.where(here, j, 0)
+
+        return pl.BlockSpec((None, length, columns), index)
+
     return pl.pallas_call(
         bands_kernel,
         out_shape=jax.ShapeDtypeStruct((3, width, regions), jnp.float32),
@@ -757,23 +791,25 @@
                 pl.BlockSpec((3, length, width), lambda j, at: (0, 0, at[1]), pipeline_mode=pl.Buffered(1)),
                 pl.BlockSpec(weights.shape, lambda j, at: (0, 0)),
                 pl.BlockSpec(prior.shape, lambda j, at: (0, 0)),
-                pl.BlockSpec((slots, length, columns), lambda j, at: (0, 0, j)),
+                *[right(slot) for slot in range(slots)],
             ],
             out_specs=pl.BlockSpec((3, width, columns), lambda j, at: (0, 0, j)),
-            scratch_shapes=[pltpu.VMEM((len(PRODUCTS), width, length), full.dtype)],
+            scratch_shapes=[pltpu.VMEM((6, width, length), full.dtype)],
         ),
         compiler_params=pltpu.CompilerParams(dimension_semantics=("arbitrary",), vmem_limit_bytes=60 << 20),
         cost_estimate=pl.CostEstimate(
             flops=10 * width * length * regions, bytes_accessed=full.size * 2 + 12 * width * regions,
             transcendentals=0),
-    )(at, full, weights, prior, full)
-
-
-def schur_kernel(at_ref, left_ref, weight_ref, prior_ref, inner_ref, full_ref, out_ref, turned):
-    week, mine = at_ref[0], at_ref[1]
+    )(at, full, weights, prior, *[full] * slots)
+
+
+def schur_kernel(at_ref, left_ref, weight_ref, prior_ref, inner_ref, *refs):
+    full_refs, out_refs, turned, total = refs[:3], refs[3:-2], refs[-2], refs[-1]
+    week = at_ref[0]
     tile = pl.program_id(0)
     slots, length, width = left_ref.shape
-    columns = full_ref.shape[2]
+    columns = total.shape[1]
+    tiles = pl.num_programs(0) // len(out_refs)
 
     @pl.when(week == 1)
     def _():
@@ -787,23 +823,38 @@
                     flat = flat - inner * weight_ref[3 + k][None, :]
                 turned[k] = flat.astype(turned.dtype)
 
-        total = jnp.dot(turned[0], full_ref[0], preferred_element_type=jnp.float32)
+        block = jnp.dot(turned[0], full_refs[0][...], preferred_element_type=jnp.float32)
         for k in range(1, slots):
-            total = total + jnp.dot(turned[k], full_ref[k], preferred_element_type=jnp.float32)
-        row_ids = lax.broadcasted_iota(jnp.int32, (width, columns), 0) + mine * width
-        col_ids = lax.broadcasted_iota(jnp.int32, (width, columns), 1) + tile * columns
-        total = total + jnp.where(row_ids == col_ids, prior_ref[:, :1], 0.0)
-        out_ref[...] = total.astype(out_ref.dtype)
-
-
-def schur_rows(at, full, weights, prior, inner):
+            block = block + jnp.dot(turned[k], full_refs[k][...], preferred_element_type=jnp.float32)
+        total[...] = block
+
+        def add(at):
+            total[:, at] += diagonal(prior_ref, width)
+
+        when_tile(at_ref, tile, columns, width, add)
+        for q, out_ref in enumerate(out_refs):
+            @pl.when(tile // tiles == q)
+            def _(out_ref=out_ref):
+                out_ref[...] = total[...].astype(out_ref.dtype)
+
+
+def schur_rows(at, full, weights, prior, inner, columns):
     _, length, regions = full.shape
     width = prior.shape[0]
-    columns = min(512, regions)
+    quarters = 4
+    columns = min(columns, regions // quarters)
+    tiles = regions // quarters // columns
     whole = pl.Buffered(1)
+
+    def part(q):
+        return pl.BlockSpec((width, columns), lambda j, at: (0, jnp.clip(j - q * tiles, 0, tiles - 1)))
+
+    def right(slot):
+        return pl.BlockSpec((None, length, columns), lambda j, at: (slot, 0, jnp.where(at[0] == 1, j, 0)))
+
     return pl.pallas_call(
         schur_kernel,
-        out_shape=jax.ShapeDtypeStruct((width, regions), jnp.bfloat16),
+        out_shape=[jax.ShapeDtypeStruct((width, regions // quarters), jnp.bfloat16)] * quarters,
         grid_spec=pltpu.PrefetchScalarGridSpec(
             num_scalar_prefetch=1,
             grid=(regions // columns,),
@@ -812,15 +863,15 @@
                 pl.BlockSpec(weights.shape, lambda j, at: (0, 0)),
                 pl.BlockSpec(prior.shape, lambda j, at: (0, 0)),
                 pl.BlockSpec(inner.shape, lambda j, at: (0, 0, 0), pipeline_mode=whole),
-                pl.BlockSpec((3, length, columns), lambda j, at: (0, 0, jnp.where(at[0] == 1, j, 0))),
+                *[right(slot) for slot in range(3)],
             ],
-            out_specs=pl.BlockSpec((width, columns), lambda j, at: (0, j)),
-            scratch_shapes=[pltpu.VMEM((3, width, length), full.dtype)],
+            out_specs=[part(q) for q in range(quarters)],
+            scratch_shapes=[pltpu.VMEM((3, width, length), full.dtype), pltpu.VMEM((width, columns), jnp.float32)],
         ),
         compiler_params=pltpu.CompilerParams(dimension_semantics=("arbitrary",), vmem_limit_bytes=60 << 20),
         cost_estimate=pl.CostEstimate(
             flops=6 * width * length * regions, bytes_accessed=6 * length * regions, transcendentals=0),
-    )(at, full, weights, prior, inner, full)
+    )(at, full, weights, prior, inner, *[full] * 3)
 
 
 def body(sensitivity, reach, obs_weight, prior_precision, pivot_solve):
@@ -840,11 +891,11 @@
 
     at = jnp.stack([week, mine]).astype(jnp.int32)
     prior = jnp.broadcast_to(prior_precision[0][:, None], (width, 128))
-    out = schur_rows(at, full, weights, prior, inner)
-    quarter = out.shape[1] // n_week
-    schur = out[:, quarter : 2 * quarter]
-    moved = [(w, lax.ppermute(out[:, w * quarter : (w + 1) * quarter], WEEK, [(1, w)])) for w in (2, 3, 0)]
-    h = bands(at, full, weights, prior)
+    columns = max(min(1024, full.shape[2] // n_week), width)
+    rows = schur_rows(at, full, weights, prior, inner, columns)
+    moved = [(w, lax.ppermute(rows[w], WEEK, [(1, w)])) for w in (2, 3, 0)]
+    h = bands(at, full, weights, prior, max(min(512, full.shape[2] // n_week), width))
+    schur = rows[1]
     for w, block in moved:
         schur = jnp.where(week == w, block, schur)
     return (h[None], panel, schur.astype(jnp.float32))

time: 348 us -> 340 us (0.977)
  local copies, waits for them, and re-layouts: 6.9 us -> 3.42 us
    pallas_call x1, Pallas kernels: 39 us -> 34.3 us  [bands(): pl.pallas_call(bands_kernel, out_shape=jax.ShapeDtypeStruct((3, width, re...]
    slice x1 -> x0, local copies, waits for them, and re-layouts: 3.48 us -> none  [body(): out[:, w * quarter:(w + 1) * quarter]]
  transfers between devices with their start and end apart: 3 -> 3, of which waited for: 0 -> 0; matrix products, arithmetic and copies ran while one was open for 0% -> 0% of each run, Pallas kernels for 11% -> 10%
where the time goes in v4:
time: 340 us
  Pallas kernels  327 us (96%)
  starting transfers between devices  4.97 us (1%)
  other arithmetic  3.54 us (1%)
  local copies, waits for them, and re-layouts  3.42 us (1%)
    pallas_call x1, Pallas kernels, gather(): pl.pallas_call(functools.partial(gather_kernel, n_row, n_col), out_shape=...  269 us
    pallas_call x1, Pallas kernels, bands(): pl.pallas_call(bands_kernel, out_shape=jax.ShapeDtypeStruct((3, width, re...  34.3 us
    pallas_call x1, Pallas kernels, schur_rows(): pl.pallas_call(schur_kernel, out_shape=[jax.ShapeDtypeStruct((width, regi...  24.5 us
  transfers between devices with their start and end apart: 3, of which 0 were waited for; matrix products, arithmetic and copies ran while one was open for 0% of the time, Pallas kernels for 10%

profile of v4, /device:TPU:5, one launch (start us, length us, event | category | flops | bytes accessed | tf_op | source)
XLA Modules:
  0.0 340.0 jit_solution(16343322177867133852)
XLA Ops:
  0.6 0.0 copy-start.2
  0.7 1.4 fusion.2.weight_ref
  2.1 268.6 %shard_map.76 = (bf16[5,1024,4096]{2,1,0:T(8,128)(2,1)}, bf16[512,1024]{1,0:T(8,128)(2,1)}, bf16[2,512,2048]{2,1,0:T(8,128)(2,1)}, f32[4,8,1024]{2,1,0:T(8,128)}) custom-call(bf16[3,1024,512]{2,1,0:T(8,128)(2,1)} %bitcast.20, bf16[1024,512]{1,0:T(8,128)(2,1)} %pivot_ref.1, f32[8,1024]{1,0:T(8,128)} %fusion.2.weight_ref), custom_call_target="tpu_custom_call" | custom-call | bytes 132120576 | tf_op jit(solution)/shard_map/pallas_call | solution.py:686
  270.7 0.9 slice.21
  271.6 0.6 pad_add_fusion.at_ref
  272.2 0.6 stack.15.weight_ref
  272.9 0.0 copy-done.2
  272.9 0.8 broadcast_in_dim.30.prior_ref
  273.7 24.5 %shard_map.78 = (bf16[512,1024]{1,0:T(8,128)(2,1)}, bf16[512,1024]{1,0:T(8,128)(2,1)}, bf16[512,1024]{1,0:T(8,128)(2,1)}, bf16[512,1024]{1,0:T(8,128)(2,1)}) custom-call(s32[2]{0:T(128)} %pad_add_fusion.at_ref, bf16[5,1024,4096]{2,1,0:T(8,128)(2,1)} %get-tuple-element.11.left_ref.refs_0_.refs_1_.refs_2_.refs_3_.refs_4_, f32[6,1024]{1,0:T(8,128)} %stack.15.weight_ref, ...), custom_call_target="tpu_custom_call" | custom-call | flops 12884901888 | bytes 25165824 | tf_op jit(solution)/shard_map/pallas_call | solution.py:855
  298.2 1.3 collective-permute-start
  299.5 1.4 collective-permute-start.1
  300.9 2.3 collective-permute-start.2
  303.2 0.0 copy-start.1
  303.2 34.3 %shard_map.77 = f32[3,512,4096]{2,1,0:T(8,128)} custom-call(s32[2]{0:T(128)} %pad_add_fusion.at_ref, bf16[5,1024,4096]{2,1,0:T(8,128)(2,1)} %get-tuple-element.11.left_ref.refs_0_.refs_1_.refs_2_.refs_3_.refs_4_, f32[6,1024]{1,0:T(8,128)} %stack.15.weight_ref, f32[512,128]{1,0:T(8,128)} %broadcast_in_dim.30.prior_ref, ...), custom_call_target="tpu_custom_call" | custom-call | flops 21474836480 | bytes 67108864 | tf_op jit(solution)/shard_map/pallas_call | solution.py:784
  337.5 0.0 copy-start
  337.5 0.0 collective-permute-done
  337.5 0.0 collective-permute-done.1
  337.5 0.0 collective-permute-done.2
  337.5 0.0 copy-done.1
  337.5 1.6 select_convert_fusion
  339.1 0.0 copy-done
  339.1 1.0 copy.9
  (2 shorter events, 0.0 us)
Async XLA Ops:
  0.6 272.2 %copy-start.2 = (f32[1,512]{1,0:T(1,128)S(1)}, f32[1,512]{1,0:T(1,128)}, u32[]{:S(2)}) copy-start(f32[1,512]{1,0:T(1,128)} %param.8) | copy-start | bytes 6148
  298.2 39.3 %collective-permute-start = (bf16[512,1024]{1,0:T(8,128)(2,1)}, bf16[512,1024]{1,0:T(8,128)(2,1)S(1)}, u32[]{:S(2)}, u32[]{:S(2)}) collective-permute-start(bf16[512,1024]{1,0:T(8,128)(2,1)} %get-tuple-element.15), channel_id=1, source_target_pairs={{8,0},{9,1},{10,2},{11,3},{12,4},{13,5},{14,6},{15,7}} | collective-permute-start | bytes 3145736 | tf_op jit(solution)/shard_map/ppermute | solution.py:896
  299.5 37.9 %collective-permute-start.1 = (bf16[512,1024]{1,0:T(8,128)(2,1)}, bf16[512,1024]{1,0:T(8,128)(2,1)S(1)}, u32[]{:S(2)}, u32[]{:S(2)}) collective-permute-start(bf16[512,1024]{1,0:T(8,128)(2,1)} %get-tuple-element.16), channel_id=1, source_target_pairs={{8,24},{9,25},{10,26},{11,27},{12,28},{13,29},{14,30},{15,31}} | collective-permute-start | bytes 3145736 | tf_op jit(solution)/shard_map/ppermute | solution.py:896
  300.9 36.6 %collective-permute-start.2 = (bf16[512,1024]{1,0:T(8,128)(2,1)}, bf16[512,1024]{1,0:T(8,128)(2,1)}, u32[]{:S(2)}, u32[]{:S(2)}) collective-permute-start(bf16[512,1024]{1,0:T(8,128)(2,1)} %get-tuple-element.17), channel_id=1, source_target_pairs={{8,16},{9,17},{10,18},{11,19},{12,20},{13,21},{14,22},{15,23}} | collective-permute-start | bytes 3145736 | tf_op jit(solution)/shard_map/ppermute | solution.py:896
  303.2 34.3 %copy-start.1 = (bf16[512,1024]{1,0:T(8,128)(2,1)S(1)}, bf16[512,1024]{1,0:T(8,128)(2,1)}, u32[]{:S(2)}) copy-start(bf16[512,1024]{1,0:T(8,128)(2,1)} %get-tuple-element.18) | copy-start | bytes 3145732
  337.5 1.6 copy-start

commit v5 on v4

--- a/solution.py
+++ b/solution.py
@@ -11,6 +11,8 @@
 DMA = pltpu.SemaphoreType.DMA
 
 UNITS = 5
+ALL, MIDDLE, EDGE = range(3)
+ORDER = ((0, ALL), (1, ALL), (2, MIDDLE), (4, EDGE), (2, EDGE), (3, ALL))
 UNIT_SLOT = ((0, 0, 0, 0), (0, 0, 0, 0), (1, 1, 3, 3), (1, 2, 2, 3), (2, 0, 0, 2))
 UNIT_HALF = ((0, 0, 0, 0), (1, 1, 1, 1), (0, 0, 1, 0), (1, 0, 1, 1), (0, 0, 0, 1))
 LOCAL = {
@@ -31,6 +33,16 @@
 FLOWS = 6
 
 
+TERMS = (
+    (((0, 0, 0), (1, 1, 1), (2, 2, 2)), (), ()),
+    (((0, 0, 0), (1, 1, 1), (2, 2, 2)), ((0, 3, 3), (1, 4, 4)), ()),
+    (((0, 0, 0), (1, 1, 1)), ((0, 3, 3), (1, 4, 4)), ((0, 2, 5),)),
+    (((0, 0, 0),), ((0, 3, 3),), ((0, 2, 5),)),
+)
+HAVE = tuple(tuple(any(right == slot for band in week for _, right, _ in band) for week in TERMS) for slot in range(5))
+SCALE = ((0, 0), (1, 1), (2, 2), (0, 1), (1, 2), (0, 2))
+
+
 def pick(week, values):
     out = jnp.int32(values[0])
     for k, value in enumerate(values[1:], 1):
@@ -42,11 +54,11 @@
     return lax.dot_general(left, right, (((1,), (1,)), ((), ())), preferred_element_type=jnp.float32)
 
 
-def gather_kernel(n_row, n_col, x_ref, pivot_ref, weight_ref, f_ref, panel_ref, inner_ref, weights_ref,
+def gather_kernel(n_row, n_col, x_ref, pivot_ref, weight_ref, f_ref, panel_ref, inner_ref, left_ref,
                   own, put_sem, first_s, first_r, z_s, z_r, pair_s, cross_s, cross_r, y_s, y_r, flow_s, flow_r,
                   low, piv, high, part, came_z, came_y, whole, turned, pan, inn, inn_in, wall,
                   low_s, low_r, piv_s, piv_r, high_s, high_r, loc, half_s, half_r, sum_s, sum_r,
-                  all_s, all_r, back_s, back_r, pan_s, pan_r, inn_s, inn_r, wt_s, wt_r):
+                  all_s, all_r, back_s, back_r, pan_s, pan_r, inn_s, inn_r, wt_s, wt_r, flat, left, left_s):
     row, col, week = lax.axis_index(ROW), lax.axis_index(COL), lax.axis_index(WEEK)
     _, length, width = x_ref.shape
     half = length // 2
@@ -92,6 +104,12 @@
         else:
             pl.when(edge)(body)
 
+    def during(item, body):
+        if item[1] == ALL:
+            body(item[0])
+        else:
+            pl.when(middle if item[1] == MIDDLE else edge)(functools.partial(body, item[0]))
+
     def other(k):
         return lax.rem(col + n_col - k, n_col)
 
@@ -311,12 +329,40 @@
     def column(slot, s):
         return f_ref.at[slot, :, pl.ds(pl.multiple_of(s * width, width), width)]
 
+    def flow_in(flow, s):
+        remote(cell(0, 0, s), flow_s.at[0, s], flow_r.at[flow, s], {ROW: pair}).wait_recv()
+
+    def own_flows():
+        @pl.when(middle)
+        def _():
+            for flow in range(FLOWS - 1):
+                flow_in(flow, mine)
+
+    def left_out():
+        return pltpu.make_async_copy(left, left_ref, left_s.at[3])
+
+    def turn_left():
+        for k in range(1, n_week):
+            weight_copy(k).wait_recv()
+        own_weight().wait()
+        for w, by_band in enumerate(TERMS):
+            @pl.when(week == w)
+            def _(w=w, by_band=by_band):
+                items = [item for band in by_band for item in band]
+                slots_used = sorted({slot for slot, _, _ in items})
+                for slot in slots_used:
+                    pltpu.make_async_copy(column(slot, mine), flat.at[slot], left_s.at[slot]).start()
+                for slot in slots_used:
+                    pltpu.make_async_copy(column(slot, mine), flat.at[slot], left_s.at[slot]).wait()
+                for slot, _, p in items:
+                    lag = SCALE[p][0]
+                    scale = wall[w + lag, SCALE[p][1], :]
+                    left[p] = (flat[slot].T.astype(jnp.float32) * scale[None, :]).astype(left.dtype)
+
+        left_out().start()
+
     def start_high():
-        @pl.when(middle)
-        def _():
-            for s in slabs:
-                ref = cell(0, 0, s)
-                remote(ref, flow_s.at[0, s], flow_r.at[3, s], {ROW: pair}).wait_recv()
+        pl.when(middle)(lambda: flow_in(3, far))
 
         @pl.when(week == 1)
         def _():
@@ -370,9 +416,6 @@
 
     def turn_high():
         wait_high()
-        for k in range(1, n_week):
-            weight_copy(k).wait_recv()
-        own_weight().wait()
         step = min(length, 512)
         for j in range(2):
             for op in range(2):
@@ -410,7 +453,11 @@
         @pl.when(middle)
         def _():
             inner_near(j).wait_recv()
-            inn[j] = (inn[j].astype(jnp.float32) + inn_in[j].astype(jnp.float32)).astype(inn.dtype)
+            for op in range(2):
+                at = op_rows(op)
+                both = inn[j, :, at].astype(jnp.float32) + inn_in[j, :, at].astype(jnp.float32)
+                inn[j, :, at] = (both * wall[1 + op, 1 + op, :][None, :]).astype(inn.dtype)
+
             pl.when(week == 2)(lambda: inner_far(j, 1).start())
 
             @pl.when(week == 1)
@@ -431,143 +478,155 @@
 
         local(u, move)
 
-    for u in range(UNITS):
-        local(u, lambda w, u=u: put(u).wait())
+    def begin(u):
+        local(u, lambda w: put(u).wait())
         for _, _, _, week_of, unit in FIRST:
             if unit == u:
                 @pl.when(week == week_of)
-                def _(u=u):
+                def _():
                     remote(place(u, mine), first_s.at[u], first_r.at[u], {ROW: pair}).wait_recv()
 
-        def begin(u=u):
-            @pl.when(inside)
-            def _():
-                to_opp(u, mine, 0).start()
-                to_pair(u, mine, 0).start()
-
-            pl.when(outside)(lambda: to_pair(u, mine, 1).start())
-            aside(u, mine, 0)
-
-        active(u, begin)
-        pl.when(outside)(lambda u=u: spread(u, mine))
-
-    def from_side(u, at_row, hop, onward=None):
-        def body():
+        @pl.when(inside)
+        def _():
+            to_opp(u, mine, 0).start()
+            to_pair(u, mine, 0).start()
+
+        pl.when(outside)(lambda: to_pair(u, mine, 1).start())
+        aside(u, mine, 0)
+        pl.when(outside)(lambda: spread(u, mine))
+
+    for item in ORDER:
+        during(item, begin)
+
+    def from_side(item, at_row, hop, onward=None):
+        def body(u):
             for k in peers:
                 side(u, mine, hop, k).wait_recv()
                 if onward is not None:
-                    onward(k)
+                    onward(u, k)
                 spread(u, slab(at_row, other(k)))
 
-        active(u, body)
-
-    def arrived(u, s, hop, then):
-        def body():
+        during(item, body)
+
+    def arrived(item, s, hop, then):
+        def body(u):
             to_pair(u, s, hop).wait_recv()
-            then()
+            then(u)
             spread(u, s)
 
-        active(u, body)
+        during(item, body)
 
     @pl.when(outside)
     def _():
-        for u in range(UNITS):
-            from_side(u, row, 0, lambda k, u=u: cross(u, k).start())
+        for item in ORDER:
+            from_side(item, row, 0, lambda u, k: cross(u, k).start())
         for hop, at_row in enumerate((pair, opp, end)):
             s = slab(at_row, col)
-            for u in range(UNITS):
-                arrived(u, s, hop, lambda u=u, s=s, hop=hop: aside(u, s, hop + 1))
+            for i, item in enumerate(ORDER):
+                arrived(item, s, hop, lambda u, s=s, hop=hop: aside(u, s, hop + 1))
                 if hop:
-                    from_side(u, (pair, opp)[hop - 1], hop)
-                if hop == 2 and u == 2:
+                    from_side(item, (pair, opp)[hop - 1], hop)
+                if hop == 2 and i == 3:
                     relays(row)
                     relays(pair)
-        for u in range(UNITS):
-            from_side(u, end, 3)
+                    own_flows()
+                    turn_left()
+                if hop == 2 and i >= 2:
+                    from_side(ORDER[i - 2], end, 3)
         relays(opp)
+        for item in ORDER[-2:]:
+            from_side(item, end, 3)
         relays(end)
 
     @pl.when(inside)
     def _():
-        def cross_in(u):
-            def body():
+        def cross_in(item):
+            def body(u):
                 for k in peers:
                     cross(u, k).wait_recv()
                     spread(u, slab(pair, other(k)))
 
-            active(u, body)
-
-        def near_one(u):
-            s = slab(opp, col)
-
-            def then():
-                to_pair(u, s, 1).start()
-                aside(u, s, 1)
-
-            arrived(u, s, 0, then)
-
-        def far_one(u):
-            s = slab(end, col)
-
-            def then():
-                to_pair(u, s, 2).start()
-                aside(u, s, 2)
-
-            arrived(u, s, 2, then)
-
-        def pass_on(u):
-            active(u, lambda: to_opp(u, far, 2).start())
-
-        def outer_one(u):
-            arrived(u, far, 1, lambda: None)
-
-        near_one(0)
-        near_one(1)
+            during(item, body)
+
+        def hand(item, at_row, hop):
+            s = slab(at_row, col)
+
+            def then(u):
+                to_pair(u, s, hop).start()
+                aside(u, s, hop)
+
+            arrived(item, s, 2 * hop - 2, then)
+
+        def near_one(item):
+            hand(item, opp, 1)
+
+        def far_one(item):
+            hand(item, end, 2)
+
+        def pass_on(item):
+            during(item, lambda u: to_opp(u, far, 2).start())
+
+        def outer_one(item):
+            arrived(item, far, 1, lambda u: None)
+
+        start, middle_part, last = ORDER[:2], ORDER[2:4], ORDER[4:]
+        for item in start:
+            near_one(item)
         spread_low()
         make_part()
-        for u in range(UNITS):
-            spread(u, mine)
-        near_one(2)
-        for u in range(2):
-            outer_one(u)
-            pass_on(u)
+        for item in ORDER:
+            during(item, lambda u: spread(u, mine))
+        for item in middle_part:
+            near_one(item)
+        for item in start:
+            outer_one(item)
+            pass_on(item)
         for k in peers:
             add_half(k)
-        for u in range(3, UNITS):
-            near_one(u)
-        for u in range(2, UNITS):
-            outer_one(u)
-        for u in range(UNITS):
-            from_side(u, row, 0)
+        for item in last:
+            near_one(item)
+        for item in (*middle_part, *last):
+            outer_one(item)
+        for item in ORDER:
+            from_side(item, row, 0)
         add_half(0)
         make_whole()
-        far_one(0)
-        pass_on(2)
-        far_one(1)
+        far_one(start[0])
+        for item in middle_part:
+            pass_on(item)
+        far_one(start[1])
         pass_whole()
-        for u in range(3, UNITS):
-            pass_on(u)
+        for item in last:
+            pass_on(item)
+        own_flows()
         start_high()
-        for u in range(UNITS):
-            from_side(u, opp, 1)
-        for u in range(UNITS):
-            cross_in(u)
-        far_one(2)
+        for item in ORDER:
+            from_side(item, opp, 1)
+        for item in ORDER:
+            cross_in(item)
+        relays(row)
+        turn_left()
+        for item in middle_part:
+            far_one(item)
+        for item in start:
+            from_side(item, end, 2)
         turn_high()
         wait_whole()
         make_panel(1)
         make_inner(1)
+        far_one(last[0])
+        for item in middle_part:
+            from_side(item, end, 2)
         make_panel(0)
         make_inner(0)
-        for u in range(3, UNITS):
-            far_one(u)
-        relays(row)
+        for item in last[1:]:
+            far_one(item)
         relays(pair)
         join_inner(1)
         join_inner(0)
-        for u in range(UNITS):
-            from_side(u, end, 2)
         relays(opp)
+        for item in last:
+            from_side(item, end, 2)
         relays(end)
 
     @pl.when(middle)
@@ -579,7 +638,9 @@
                     remote(ref, flow_s.at[0, s], flow_r.at[flow, s], {ROW: pair}).wait_recv()
 
                 if flow == 3:
-                    pl.when(outside | ((mine != s) & (far != s)))(arrive)
+                    pl.when((mine != s) & (outside | (far != s)))(arrive)
+                elif flow < FLOWS - 1:
+                    pl.when(mine != s)(arrive)
                 else:
                     arrive()
 
@@ -591,14 +652,9 @@
     @pl.when(outside)
     def _():
         panel_out().wait_recv()
-        for k in range(1, n_week):
-            weight_copy(k).wait_recv()
-        own_weight().wait()
         by_role(lambda op, lag, *_: low_copy(x_ref.at[lag], 1, op, 0, {ROW: pair}).wait_send())
         pivot_out().wait_send()
 
-    weights_out = pltpu.make_async_copy(wall, weights_ref, wt_s.at[n_week - 1])
-    weights_out.start()
     for k in range(1, n_week):
         weight_copy(k).wait_send()
 
@@ -670,7 +726,7 @@
                 spread(u, s, "wait")
     for s in range(n):
         relay(s, "wait")
-    weights_out.wait()
+    left_out().wait()
 
 
 def gather(x, pivot, weight, collective_id):
@@ -689,7 +745,7 @@
             jax.ShapeDtypeStruct((5, length, width * n), x.dtype),
             jax.ShapeDtypeStruct((width, slices), x.dtype),
             jax.ShapeDtypeStruct((2, width, 2 * length), x.dtype),
-            jax.ShapeDtypeStruct((4, *weight.shape), weight.dtype),
+            jax.ShapeDtypeStruct((len(SCALE), width, length), x.dtype),
         ),
         in_specs=[hbm] * 3,
         out_specs=(hbm,) * 4,
@@ -707,6 +763,7 @@
             DMA((n_col,)), DMA((n_col,)), DMA((n_col - 1,)), DMA((n_col - 1,)),
             DMA((n_col - 1,)), DMA((n_col - 1,)), DMA((n_col,)), DMA((n_col,)),
             DMA((1,)), DMA((1,)), DMA((2,)), DMA((4,)), DMA((4,)), DMA((3,)),
+            vmem(3, length, width), vmem(len(SCALE), width, length), DMA((4,)),
         ],
         compiler_params=pltpu.CompilerParams(
             collective_id=collective_id, has_side_effects=True, vmem_limit_bytes=60 << 20),
@@ -714,15 +771,6 @@
     )(x, pivot, weight)
 
 
-TERMS = (
-    (((0, 0, 0), (1, 1, 1), (2, 2, 2)), (), ()),
-    (((0, 0, 0), (1, 1, 1), (2, 2, 2)), ((0, 3, 3), (1, 4, 4)), ()),
-    (((0, 0, 0), (1, 1, 1)), ((0, 3, 3), (1, 4, 4)), ((0, 2, 5),)),
-    (((0, 0, 0),), ((0, 3, 3),), ((0, 2, 5),)),
-)
-HAVE = tuple(tuple(any(right == slot for band in week for _, right, _ in band) for week in TERMS) for slot in range(5))
-
-
 def when_tile(at_ref, tile, columns, width, body):
     first = at_ref[1] * width
 
@@ -737,28 +785,21 @@
     return jnp.where(rows == cols, prior_ref[:, :1], 0.0)
 
 
-def bands_kernel(at_ref, left_ref, weight_ref, prior_ref, *refs):
-    full_refs, out_ref, turned = refs[:5], refs[5], refs[6]
+def bands_kernel(at_ref, left_ref, prior_ref, *refs):
+    full_refs, out_ref = refs[:5], refs[5]
     week = at_ref[0]
     tile = pl.program_id(0)
-    width = left_ref.shape[2]
+    width = left_ref.shape[1]
     columns = out_ref.shape[2]
 
     for w, by_band in enumerate(TERMS):
         @pl.when(week == w)
         def _(by_band=by_band):
-            @pl.when(tile == 0)
-            def _():
-                for band in by_band:
-                    for slot, _, p in band:
-                        flat = left_ref[slot].T.astype(jnp.float32) * weight_ref[p][None, :]
-                        turned[p] = flat.astype(turned.dtype)
-
             for i, band in enumerate(by_band):
                 if band:
                     total = None
                     for _, right, p in band:
-                        term = jnp.dot(turned[p], full_refs[right][...], preferred_element_type=jnp.float32)
+                        term = jnp.dot(left_ref[p], full_refs[right][...], preferred_element_type=jnp.float32)
                         total = term if total is None else total + term
                     out_ref[i] = total
                 else:
@@ -770,7 +811,7 @@
     when_tile(at_ref, tile, columns, width, add)
 
 
-def bands(at, full, weights, prior, columns):
+def bands(at, full, left, prior, columns):
     slots, length, regions = full.shape
     width = prior.shape[0]
 
@@ -788,26 +829,24 @@
             num_scalar_prefetch=1,
             grid=(regions // columns,),
             in_specs=[
-                pl.BlockSpec((3, length, width), lambda j, at: (0, 0, at[1]), pipeline_mode=pl.Buffered(1)),
-                pl.BlockSpec(weights.shape, lambda j, at: (0, 0)),
+                pl.BlockSpec(left.shape, lambda j, at: (0, 0, 0), pipeline_mode=pl.Buffered(1)),
                 pl.BlockSpec(prior.shape, lambda j, at: (0, 0)),
                 *[right(slot) for slot in range(slots)],
             ],
             out_specs=pl.BlockSpec((3, width, columns), lambda j, at: (0, 0, j)),
-            scratch_shapes=[pltpu.VMEM((6, width, length), full.dtype)],
         ),
         compiler_params=pltpu.CompilerParams(dimension_semantics=("arbitrary",), vmem_limit_bytes=60 << 20),
         cost_estimate=pl.CostEstimate(
             flops=10 * width * length * regions, bytes_accessed=full.size * 2 + 12 * width * regions,
             transcendentals=0),
-    )(at, full, weights, prior, *[full] * slots)
-
-
-def schur_kernel(at_ref, left_ref, weight_ref, prior_ref, inner_ref, *refs):
+    )(at, left, prior, *[full] * slots)
+
+
+def schur_kernel(at_ref, left_ref, prior_ref, inner_ref, *refs):
     full_refs, out_refs, turned, total = refs[:3], refs[3:-2], refs[-2], refs[-1]
     week = at_ref[0]
     tile = pl.program_id(0)
-    slots, length, width = left_ref.shape
+    slots, width, length = left_ref.shape
     columns = total.shape[1]
     tiles = pl.num_programs(0) // len(out_refs)
 
@@ -815,17 +854,14 @@
     def _():
         @pl.when(tile == 0)
         def _():
-            for k in range(slots):
-                flat = left_ref[k].T.astype(jnp.float32) * weight_ref[k][None, :]
-                if k < 2:
-                    at = pl.ds(k * length, length)
-                    inner = inner_ref[0, :, at].astype(jnp.float32) + inner_ref[1, :, at].astype(jnp.float32)
-                    flat = flat - inner * weight_ref[3 + k][None, :]
-                turned[k] = flat.astype(turned.dtype)
+            for k in range(2):
+                at = pl.ds(k * length, length)
+                inner = inner_ref[0, :, at].astype(jnp.float32) + inner_ref[1, :, at].astype(jnp.float32)
+                turned[k] = (left_ref[k].astype(jnp.float32) - inner).astype(turned.dtype)
 
         block = jnp.dot(turned[0], full_refs[0][...], preferred_element_type=jnp.float32)
-        for k in range(1, slots):
-            block = block + jnp.dot(turned[k], full_refs[k][...], preferred_element_type=jnp.float32)
+        block = block + jnp.dot(turned[1], full_refs[1][...], preferred_element_type=jnp.float32)
+        block = block + jnp.dot(left_ref[2], full_refs[2][...], preferred_element_type=jnp.float32)
         total[...] = block
 
         def add(at):
@@ -838,7 +874,7 @@
                 out_ref[...] = total[...].astype(out_ref.dtype)
 
 
-def schur_rows(at, full, weights, prior, inner, columns):
+def schur_rows(at, full, left, prior, inner, columns):
     _, length, regions = full.shape
     width = prior.shape[0]
     quarters = 4
@@ -859,19 +895,18 @@
             num_scalar_prefetch=1,
             grid=(regions // columns,),
             in_specs=[
-                pl.BlockSpec((3, length, width), lambda j, at: (0, 0, at[1]), pipeline_mode=whole),
-                pl.BlockSpec(weights.shape, lambda j, at: (0, 0)),
+                pl.BlockSpec((3, width, length), lambda j, at: (0, 0, 0), pipeline_mode=whole),
                 pl.BlockSpec(prior.shape, lambda j, at: (0, 0)),
                 pl.BlockSpec(inner.shape, lambda j, at: (0, 0, 0), pipeline_mode=whole),
                 *[right(slot) for slot in range(3)],
             ],
             out_specs=[part(q) for q in range(quarters)],
-            scratch_shapes=[pltpu.VMEM((3, width, length), full.dtype), pltpu.VMEM((width, columns), jnp.float32)],
+            scratch_shapes=[pltpu.VMEM((2, width, length), full.dtype), pltpu.VMEM((width, columns), jnp.float32)],
         ),
         compiler_params=pltpu.CompilerParams(dimension_semantics=("arbitrary",), vmem_limit_bytes=60 << 20),
         cost_estimate=pl.CostEstimate(
             flops=6 * width * length * regions, bytes_accessed=6 * length * regions, transcendentals=0),
-    )(at, full, weights, prior, inner, *[full] * 3)
+    )(at, left, prior, inner, *[full] * 3)
 
 
 def body(sensitivity, reach, obs_weight, prior_precision, pivot_solve):
@@ -883,18 +918,13 @@
 
     lag = jnp.arange(8)[:, None]
     own_weight = jnp.where((reach >= lag) & (week >= lag) & (lag < lags), obs_weight, 0.0)
-    full, panel, inner, by_week = gather(local, pivot_solve, own_weight, 0)
-    by_week = by_week[:, :lags]
-    later = jnp.concatenate([by_week, jnp.zeros((lags, lags, length), by_week.dtype)])
-    here = lax.dynamic_slice(later, (week, 0, 0), (lags, lags, length))
-    weights = jnp.stack([here[0, 0], here[1, 1], here[2, 2], here[0, 1], here[1, 2], here[0, 2]])
-
+    full, panel, inner, left = gather(local, pivot_solve, own_weight, 0)
     at = jnp.stack([week, mine]).astype(jnp.int32)
     prior = jnp.broadcast_to(prior_precision[0][:, None], (width, 128))
     columns = max(min(1024, full.shape[2] // n_week), width)
-    rows = schur_rows(at, full, weights, prior, inner, columns)
+    rows = schur_rows(at, full, left, prior, inner, columns)
     moved = [(w, lax.ppermute(rows[w], WEEK, [(1, w)])) for w in (2, 3, 0)]
-    h = bands(at, full, weights, prior, max(min(512, full.shape[2] // n_week), width))
+    h = bands(at, full, left, prior, max(min(512, full.shape[2] // n_week), width))
     schur = rows[1]
     for w, block in moved:
         schur = jnp.where(week == w, block, schur)

time: 340 us -> 321 us (0.944)
  Pallas kernels: 327 us -> 309 us
    pallas_call x1, Pallas kernels: 269 us -> 252 us  [gather(): pl.pallas_call(functools.partial(gather_kernel, n_row, n_col), out_shape=...]
  transfers between devices with their start and end apart: 3 -> 3, of which waited for: 0 -> 0; matrix products, arithmetic and copies ran while one was open for 0% -> 0% of each run, Pallas kernels for 10% -> 11%
where the time goes in v5:
time: 321 us; the launch traced here: 320 us
  Pallas kernels  309 us (96%)
  starting transfers between devices  5.01 us (2%)
  other arithmetic  3.57 us (1%)
    pallas_call x1, Pallas kernels, gather(): pl.pallas_call(functools.partial(gather_kernel, n_row, n_col), out_shape=...  252 us
    pallas_call x1, Pallas kernels, bands(): pl.pallas_call(bands_kernel, out_shape=jax.ShapeDtypeStruct((3, width, re...  33.6 us
    pallas_call x1, Pallas kernels, schur_rows(): pl.pallas_call(schur_kernel, out_shape=[jax.ShapeDtypeStruct((width, regi...  23.5 us
  transfers between devices with their start and end apart: 3, of which 0 were waited for; matrix products, arithmetic and copies ran while one was open for 0% of the time, Pallas kernels for 11%

profile of v5, /device:TPU:5, one launch (start us, length us, event | category | flops | bytes accessed | tf_op | source)
XLA Modules:
  0.0 319.7 jit_solution(10722286277335402406)
XLA Ops:
  0.6 0.0 copy-start.2
  0.7 0.6 pad_add_fusion.at_ref
  1.3 1.4 fusion.2.weight_ref
  2.7 251.5 %shard_map.76 = (bf16[5,1024,4096]{2,1,0:T(8,128)(2,1)}, bf16[512,1024]{1,0:T(8,128)(2,1)}, bf16[2,512,2048]{2,1,0:T(8,128)(2,1)}, bf16[6,512,1024]{2,1,0:T(8,128)(2,1)}) custom-call(bf16[3,1024,512]{2,1,0:T(8,128)(2,1)} %bitcast.8, bf16[1024,512]{1,0:T(8,128)(2,1)} %pivot_ref.1, f32[8,1024]{1,0:T(8,128)} %fusion.2.weight_ref), custom_call_target="tpu_custom_call" | custom-call | bytes 132120576 | tf_op jit(solution)/shard_map/pallas_call | solution.py:742
  254.2 0.0 copy-done.2
  254.2 0.8 broadcast_in_dim.29.prior_ref
  255.0 23.5 %shard_map.78 = (bf16[512,1024]{1,0:T(8,128)(2,1)}, bf16[512,1024]{1,0:T(8,128)(2,1)}, bf16[512,1024]{1,0:T(8,128)(2,1)}, bf16[512,1024]{1,0:T(8,128)(2,1)}) custom-call(s32[2]{0:T(128)} %pad_add_fusion.at_ref, bf16[6,512,1024]{2,1,0:T(8,128)(2,1)} %get-tuple-element.11.left_ref, f32[512,128]{1,0:T(8,128)} %broadcast_in_dim.29.prior_ref, ...), custom_call_target="tpu_custom_call" | custom-call | flops 12884901888 | bytes 25165824 | tf_op jit(solution)/shard_map/pallas_call | solution.py:891
  278.5 1.3 collective-permute-start
  279.9 1.4 collective-permute-start.1
  281.2 2.3 collective-permute-start.2
  283.6 0.0 copy-start.1
  283.6 33.6 %shard_map.77 = f32[3,512,4096]{2,1,0:T(8,128)} custom-call(s32[2]{0:T(128)} %pad_add_fusion.at_ref, bf16[6,512,1024]{2,1,0:T(8,128)(2,1)} %get-tuple-element.11.left_ref, f32[512,128]{1,0:T(8,128)} %broadcast_in_dim.29.prior_ref, bf16[5,1024,4096]{2,1,0:T(8,128)(2,1)} %get-tuple-element.12.refs_0_.refs_1_.refs_2_.refs_3_.refs_4_, ...), custom_call_target="tpu_custom_call" | custom-call | flops 21474836480 | bytes 67108864 | tf_op jit(solution)/shard_map/pallas_call | solution.py:825
  317.2 0.0 copy-start
  317.2 0.0 collective-permute-done
  317.2 0.0 collective-permute-done.1
  317.2 0.0 collective-permute-done.2
  317.2 0.0 copy-done.1
  317.2 1.6 select_convert_fusion
  318.8 0.0 copy-done
  318.8 1.0 copy.9
  (1 shorter events, 0.0 us)
Async XLA Ops:
  0.6 253.6 %copy-start.2 = (f32[1,512]{1,0:T(1,128)S(1)}, f32[1,512]{1,0:T(1,128)}, u32[]{:S(2)}) copy-start(f32[1,512]{1,0:T(1,128)} %param.8) | copy-start | bytes 6148
  278.5 38.6 %collective-permute-start = (bf16[512,1024]{1,0:T(8,128)(2,1)}, bf16[512,1024]{1,0:T(8,128)(2,1)S(1)}, u32[]{:S(2)}, u32[]{:S(2)}) collective-permute-start(bf16[512,1024]{1,0:T(8,128)(2,1)} %get-tuple-element.15), channel_id=1, source_target_pairs={{8,0},{9,1},{10,2},{11,3},{12,4},{13,5},{14,6},{15,7}} | collective-permute-start | bytes 3145736 | tf_op jit(solution)/shard_map/ppermute | solution.py:926
  279.9 37.3 %collective-permute-start.1 = (bf16[512,1024]{1,0:T(8,128)(2,1)}, bf16[512,1024]{1,0:T(8,128)(2,1)S(1)}, u32[]{:S(2)}, u32[]{:S(2)}) collective-permute-start(bf16[512,1024]{1,0:T(8,128)(2,1)} %get-tuple-element.16), channel_id=1, source_target_pairs={{8,24},{9,25},{10,26},{11,27},{12,28},{13,29},{14,30},{15,31}} | collective-permute-start | bytes 3145736 | tf_op jit(solution)/shard_map/ppermute | solution.py:926
  281.2 35.9 %collective-permute-start.2 = (bf16[512,1024]{1,0:T(8,128)(2,1)}, bf16[512,1024]{1,0:T(8,128)(2,1)}, u32[]{:S(2)}, u32[]{:S(2)}) collective-permute-start(bf16[512,1024]{1,0:T(8,128)(2,1)} %get-tuple-element.17), channel_id=1, source_target_pairs={{8,16},{9,17},{10,18},{11,19},{12,20},{13,21},{14,22},{15,23}} | collective-permute-start | bytes 3145736 | tf_op jit(solution)/shard_map/ppermute | solution.py:926
  283.6 33.6 %copy-start.1 = (bf16[512,1024]{1,0:T(8,128)(2,1)S(1)}, bf16[512,1024]{1,0:T(8,128)(2,1)}, u32[]{:S(2)}) copy-start(bf16[512,1024]{1,0:T(8,128)(2,1)} %get-tuple-element.18) | copy-start | bytes 3145732
  317.2 1.6 copy-start

commit v6 on v5

--- a/solution.py
+++ b/solution.py
@@ -439,7 +439,7 @@
         if j == 0:
             local_copy(pan.at[0], panel_ref, 0).start()
         else:
-            panel_out().start()
+            pl.when(middle)(lambda: panel_out().start())
 
     def make_inner(j):
         @pl.loop(0, 2 * length // tile)
@@ -621,6 +621,7 @@
         make_inner(0)
         for item in last[1:]:
             far_one(item)
+        pl.when(edge)(lambda: panel_out().start())
         relays(pair)
         join_inner(1)
         join_inner(0)

time: 321 us -> 320 us (level)
  no operation moved by 1% of the time
where the time goes in v6:
time: 320 us; the launch traced here: 319 us
  Pallas kernels  308 us (96%)
  starting transfers between devices  5.01 us (2%)
  other arithmetic  3.57 us (1%)
    pallas_call x1, Pallas kernels, gather(): pl.pallas_call(functools.partial(gather_kernel, n_row, n_col), out_shape=...  251 us
    pallas_call x1, Pallas kernels, bands(): pl.pallas_call(bands_kernel, out_shape=jax.ShapeDtypeStruct((3, width, re...  33.6 us
    pallas_call x1, Pallas kernels, schur_rows(): pl.pallas_call(schur_kernel, out_shape=[jax.ShapeDtypeStruct((width, regi...  23.5 us
  transfers between devices with their start and end apart: 3, of which 0 were waited for; matrix products, arithmetic and copies ran while one was open for 0% of the time, Pallas kernels for 11%

profile of v6, /device:TPU:5, one launch (start us, length us, event | category | flops | bytes accessed | tf_op | source)
XLA Modules:
  0.0 319.3 jit_solution(6441437161954395802)
XLA Ops:
  0.6 0.0 copy-start.2
  0.7 0.6 pad_add_fusion.at_ref
  1.3 1.4 fusion.2.weight_ref
  2.7 251.1 %shard_map.76 = (bf16[5,1024,4096]{2,1,0:T(8,128)(2,1)}, bf16[512,1024]{1,0:T(8,128)(2,1)}, bf16[2,512,2048]{2,1,0:T(8,128)(2,1)}, bf16[6,512,1024]{2,1,0:T(8,128)(2,1)}) custom-call(bf16[3,1024,512]{2,1,0:T(8,128)(2,1)} %bitcast.8, bf16[1024,512]{1,0:T(8,128)(2,1)} %pivot_ref.1, f32[8,1024]{1,0:T(8,128)} %fusion.2.weight_ref), custom_call_target="tpu_custom_call" | custom-call | bytes 132120576 | tf_op jit(solution)/shard_map/pallas_call | solution.py:743
  253.8 0.0 copy-done.2
  253.8 0.8 broadcast_in_dim.29.prior_ref
  254.6 23.5 %shard_map.78 = (bf16[512,1024]{1,0:T(8,128)(2,1)}, bf16[512,1024]{1,0:T(8,128)(2,1)}, bf16[512,1024]{1,0:T(8,128)(2,1)}, bf16[512,1024]{1,0:T(8,128)(2,1)}) custom-call(s32[2]{0:T(128)} %pad_add_fusion.at_ref, bf16[6,512,1024]{2,1,0:T(8,128)(2,1)} %get-tuple-element.11.left_ref, f32[512,128]{1,0:T(8,128)} %broadcast_in_dim.29.prior_ref, ...), custom_call_target="tpu_custom_call" | custom-call | flops 12884901888 | bytes 25165824 | tf_op jit(solution)/shard_map/pallas_call | solution.py:892
  278.1 1.3 collective-permute-start
  279.5 1.4 collective-permute-start.1
  280.8 2.3 collective-permute-start.2
  283.1 0.0 copy-start.1
  283.1 33.6 %shard_map.77 = f32[3,512,4096]{2,1,0:T(8,128)} custom-call(s32[2]{0:T(128)} %pad_add_fusion.at_ref, bf16[6,512,1024]{2,1,0:T(8,128)(2,1)} %get-tuple-element.11.left_ref, f32[512,128]{1,0:T(8,128)} %broadcast_in_dim.29.prior_ref, bf16[5,1024,4096]{2,1,0:T(8,128)(2,1)} %get-tuple-element.12.refs_0_.refs_1_.refs_2_.refs_3_.refs_4_, ...), custom_call_target="tpu_custom_call" | custom-call | flops 21474836480 | bytes 67108864 | tf_op jit(solution)/shard_map/pallas_call | solution.py:826
  316.8 0.0 copy-start
  316.8 0.0 collective-permute-done
  316.8 0.0 collective-permute-done.1
  316.8 0.0 collective-permute-done.2
  316.8 0.0 copy-done.1
  316.8 1.6 select_convert_fusion
  318.4 0.0 copy-done
  318.4 1.0 copy.9
  (1 shorter events, 0.0 us)
Async XLA Ops:
  0.6 253.2 %copy-start.2 = (f32[1,512]{1,0:T(1,128)S(1)}, f32[1,512]{1,0:T(1,128)}, u32[]{:S(2)}) copy-start(f32[1,512]{1,0:T(1,128)} %param.8) | copy-start | bytes 6148
  278.1 38.6 %collective-permute-start = (bf16[512,1024]{1,0:T(8,128)(2,1)}, bf16[512,1024]{1,0:T(8,128)(2,1)S(1)}, u32[]{:S(2)}, u32[]{:S(2)}) collective-permute-start(bf16[512,1024]{1,0:T(8,128)(2,1)} %get-tuple-element.15), channel_id=1, source_target_pairs={{8,0},{9,1},{10,2},{11,3},{12,4},{13,5},{14,6},{15,7}} | collective-permute-start | bytes 3145736 | tf_op jit(solution)/shard_map/ppermute | solution.py:927
  279.5 37.3 %collective-permute-start.1 = (bf16[512,1024]{1,0:T(8,128)(2,1)}, bf16[512,1024]{1,0:T(8,128)(2,1)S(1)}, u32[]{:S(2)}, u32[]{:S(2)}) collective-permute-start(bf16[512,1024]{1,0:T(8,128)(2,1)} %get-tuple-element.16), channel_id=1, source_target_pairs={{8,24},{9,25},{10,26},{11,27},{12,28},{13,29},{14,30},{15,31}} | collective-permute-start | bytes 3145736 | tf_op jit(solution)/shard_map/ppermute | solution.py:927
  280.8 35.9 %collective-permute-start.2 = (bf16[512,1024]{1,0:T(8,128)(2,1)}, bf16[512,1024]{1,0:T(8,128)(2,1)}, u32[]{:S(2)}, u32[]{:S(2)}) collective-permute-start(bf16[512,1024]{1,0:T(8,128)(2,1)} %get-tuple-element.17), channel_id=1, source_target_pairs={{8,16},{9,17},{10,18},{11,19},{12,20},{13,21},{14,22},{15,23}} | collective-permute-start | bytes 3145736 | tf_op jit(solution)/shard_map/ppermute | solution.py:927
  283.1 33.6 %copy-start.1 = (bf16[512,1024]{1,0:T(8,128)(2,1)S(1)}, bf16[512,1024]{1,0:T(8,128)(2,1)}, u32[]{:S(2)}) copy-start(bf16[512,1024]{1,0:T(8,128)(2,1)} %get-tuple-element.18) | copy-start | bytes 3145732
  316.8 1.6 copy-start
